TPU v7x, 512 devices: a whole 4x4x16 slice. The times are simulated.
512 devices in a mesh: py: 32 (over z_hi, y, core), pz: 16 (over x, z_lo).
Axes of the slice: x: 4, y: 4, z: 16 (z_hi: 4, z_lo: 4; z = z_hi * 4 + z_lo), core: 2. Of those that a mesh axis runs over, the one named last changes fastest.
Arguments:
- solution: float32 [256, 256, 512], P('py', 'pz'), may hold values from -6 to 6
- right_side: float32 [256, 256, 512], P('py', 'pz'), may hold values from -6 to 6
- span_index: int32 [256, 256, 512], P('py', 'pz'), may hold values from 0 to 7
- coef_table: float32 [8], replicated, may hold values from 0.5 to 2
- xaxis_bands: float32 [2, 7, 512], replicated, may hold values from -0.5 to 0.5
- yaxis_bands: float32 [2, 7, 256], P(None, None, 'py'), may hold values from -0.5 to 0.5
- zaxis_bands: float32 [2, 7, 256], P(None, None, 'pz'), may hold values from -0.5 to 0.5
- xaxis_vectors: float32 [512, 512], replicated, may hold values from -0.25 to 0.25
- yaxis_vectors: float32 [256, 256], replicated, may hold values from -0.375 to 0.375
- zaxis_vectors: float32 [256, 256], replicated, may hold values from -0.375 to 0.375
- xaxis_values: float32 [512], replicated, may hold values from 0.25 to 2
- yaxis_values: float32 [256], replicated, may hold values from 0.25 to 2
- zaxis_values: float32 [256], replicated, may hold values from 0.25 to 2
Outputs:
- updated: float32 [256, 256, 512], P('py', 'pz')
- residual: float32 [256, 256, 512], P('py', 'pz')
All inputs are finite; a program needn't handle non-finite values.
Results may differ from a plain program's by a relative error of at most 0.0001.
Values sent between devices are 32-bit elements; how exact they have to be, the bound alone decides.
A program may use at most 64 MiB of HBM per device.

v0:
```python
import jax
import jax.numpy as jnp
from jax import lax
from jax.experimental import pallas as pl
from jax.experimental.pallas import tpu as pltpu
from jax.sharding import PartitionSpec as P

ITERS = 2
F32 = jnp.float32
BF16 = jnp.bfloat16
RING = (8, 7, 9, 6, 10, 5, 11, 4, 12, 3, 13, 2, 14, 1, 15)


def split(v):
    hi = v.astype(BF16)
    return hi, (v - hi.astype(F32)).astype(BF16)


def dot3(a, b, dims=((1,), (0,))):
    def one(p, q):
        return lax.dot_general(p, q, (dims, ((), ())), preferred_element_type=F32)

    return one(a[0], b[0]) + one(a[0], b[1]) + one(a[1], b[0])


def swap_blocks(v, sub, lane):
    far = pltpu.roll(pltpu.roll(v, 4, 0), 64, 1)
    v = jnp.where((sub // 4) == (lane // 64), v, far)
    for bit in (2, 1):
        width = 16 * bit
        s, l = (sub // bit) % 2, (lane // width) % 2
        down = pltpu.roll(pltpu.roll(v, bit, 0), 128 - width, 1)
        up = pltpu.roll(pltpu.roll(v, 8 - bit, 0), width, 1)
        v = jnp.where(s == l, v, jnp.where(s == 1, down, up))
    return v


def kernel(
    u_in, b_in, span_in, coef, xb, yb, zb, vx_in, vy_in, vz_in, xv, yv, zv,
    u_out, r_out,
    u, b, span, vx, vy, vz, c, r, zs, cs, hr, w, acc,
    s, ra, sb, rb, m, mb, rb2, sa2, ra2,
    bm_h, bm_l, vxt_h, vxt_l, vy_h, vy_l, vyt_h, vyt_l, vz_h, vz_l, den,
    load_sem, send_sem, recv_sem,
):
    py, pz = lax.axis_index("py"), lax.axis_index("pz")
    zh, yc = py // 8, py % 8
    x, zl = pz // 4, pz % 4
    g = yc * 4 + x
    q = zh * 4 + zl

    def device(py2, pz2):
        return {"py": py2, "pz": pz2}

    def group(g2):
        return device(zh * 8 + g2 // 4, (g2 % 4) * 4 + zl)

    def ring(q2):
        return device((q2 // 4) * 8 + yc, x * 4 + q2 % 4)

    def near(dy, dz):
        return device((py + 32 + dy) % 32, (pz + 16 + dz) % 16)

    loads = [
        pltpu.make_async_copy(src, dst, load_sem.at[i])
        for i, (src, dst) in enumerate(
            ((u_in, u), (span_in, span), (vx_in, vx), (vy_in, vy), (vz_in, vz), (b_in, b))
        )
    ]
    for load in loads:
        load.start()

    barrier = pltpu.get_barrier_semaphore()

    def greet(k, carry):
        pl.semaphore_signal(barrier, inc=1, device_id=group((g + k) % 32))
        return carry

    lax.fori_loop(1, 32, greet, 0)

    def greet_ring(k, carry):
        pl.semaphore_signal(barrier, inc=1, device_id=ring((q + k) % 16))
        return carry

    lax.fori_loop(1, 16, greet_ring, 0)
    sides = [(dy, dz) for dy in (-1, 0, 1) for dz in (-1, 0, 1) if dy or dz]
    for dy, dz in sides:
        pl.semaphore_signal(barrier, inc=1, device_id=near(dy, dz))

    cs[...] = jnp.zeros_like(cs)
    for it in range(ITERS):
        hr[it, pl.ds(208, 48), :] = jnp.zeros((48, 512), F32)

    loads[0].wait()
    loads[1].wait()

    def weigh(i, carry):
        rows = pl.ds(pl.multiple_of(i * 8, 8), 8)
        at = span[rows, :]
        v = jnp.full((8, 512), coef[0], F32)
        for e in range(1, 8):
            v = jnp.where(at == e, coef[e], v)
        c[rows, :] = v
        w[0, rows, :] = v * u[rows, :]
        return carry

    lax.fori_loop(0, 16, weigh, 0)
    pl.semaphore_wait(barrier, 31 + 15 + 8)

    sub = lax.broadcasted_iota(jnp.int32, (8, 128), 0)
    lane = lax.broadcasted_iota(jnp.int32, (8, 128), 1)

    def prepare():
        def coords(tile):
            if tile == 2:
                return lane // 16, lane % 16
            col = lane + tile * 128
            yy = jnp.where(col < 48, col // 16 - 3, 8 + (col - 48) // 16)
            zz = col % 16
            k = col - 96
            edge = col >= 96
            yy = jnp.where(edge, k % 8, yy)
            zz = jnp.where(edge, jnp.where(k < 24, k // 8 - 3, 16 + (k - 24) // 8), zz)
            k = col - 144
            corner = k >= 0
            cc = k % 16
            y3 = jnp.where(cc >= 6, 2, jnp.where(cc >= 3, 1, 0))
            z3 = cc - 3 * y3
            t = k // 16
            yy = jnp.where(corner, jnp.where(t < 2, y3 - 3, 8 + y3), yy)
            zz = jnp.where(corner, jnp.where(t % 2 == 0, z3 - 3, 16 + z3), zz)
            bad = (corner & (cc >= 9)) | (col >= 208)
            gy, gz = py * 8 + yy, pz * 16 + zz
            bad = bad | (gy < 0) | (gy > 255) | (gz < 0) | (gz > 255)
            return jnp.where(bad, 1000, yy), jnp.where(bad, 1000, zz)

        for tile in range(3):
            yy, zz = coords(tile)
            ez = {}
            for half in range(2):
                dz = zz - (half * 8 + sub) + 3
                for kind in range(2):
                    total = jnp.zeros((8, 128), F32)
                    for k in range(7):
                        column = jnp.zeros((8, 128), F32)
                        for row in range(8):
                            column = jnp.where(sub == row, zb[kind, k, half * 8 + row], column)
                        total = jnp.where(dz == k, column, total)
                    ez[kind, half] = total

            def rows_of(y, carry, yy=yy, ez=ez, tile=tile):
                dy = yy - y + 3
                ey = []
                for kind in range(2):
                    total = jnp.zeros((8, 128), F32)
                    for k in range(7):
                        total = jnp.where(dy == k, yb[kind, k, y], total)
                    ey.append(total)
                mass = [ey[1] * ez[1, half] for half in range(2)]
                stiff = [ey[0] * ez[1, half] + ey[1] * ez[0, half] for half in range(2)]
                for base, pair in ((0, mass), (128, stiff)):
                    hi, lo = split(jnp.concatenate(pair, axis=0))
                    at = pl.ds(pl.multiple_of(base + y * 16, 16), 16)
                    bm_h[at, tile * 128 : tile * 128 + 128] = hi
                    bm_l[at, tile * 128 : tile * 128 + 128] = lo
                return carry

            lax.fori_loop(0, 8, rows_of, 0)
        loads[2].wait()
        for i in range(4):
            cols = slice(i * 128, i * 128 + 128)
            hi, lo = split(jnp.transpose(vx[:, cols]))
            vxt_h[cols, :] = hi
            vxt_l[cols, :] = lo
        loads[3].wait()
        vy_h[...], vy_l[...] = split(vy[...])
        vyt_h[...], vyt_l[...] = split(jnp.transpose(vy[...]))
        loads[4].wait()
        for p in range(2):
            for e in range(2):
                for xx in range(4):
                    to = p * 128 + e * 64 + xx * 16
                    at = xx * 64 + (2 * p + e) * 16
                    hi, lo = split(vz[at : at + 16, :])
                    vz_h[to : to + 16, :] = hi
                    vz_l[to : to + 16, :] = lo
        column = jnp.transpose(jnp.broadcast_to(yv[...], (128, 256)))
        j = g * 16 + q
        row = lax.broadcasted_iota(jnp.int32, (1, 512), 1)
        mine = jnp.sum(jnp.where(row == j, xv[...], 0.0), axis=1, keepdims=True)
        for half in range(2):
            cols = slice(half * 128, half * 128 + 128)
            den[:, cols] = (column + zv[:, cols]) + mine
        loads[5].wait()

    def step(it, carry):
        for i in range(3):
            for side, first in enumerate((0, 13)):
                for t in range(4):
                    cols = slice(t * 128, t * 128 + 128)
                    full = w[it, :, cols].reshape(8, 16, 128)
                    zs[it, side, i * 8 : i * 8 + 8, cols] = full[:, first + i, :]
        for cy in range(2):
            for cz in range(2):
                for i in range(3):
                    row = (cy * 5 + i) * 16 + cz * 13
                    cs[it, cy * 2 + cz, i * 3 : i * 3 + 3, :] = w[it, row : row + 3, :]
        own = w.at[it]
        rims = (
            (own.at[80:128], 0, 48, near(1, 0)),
            (own.at[0:48], 48, 48, near(-1, 0)),
            (zs.at[it, 1], 96, 24, near(0, 1)),
            (zs.at[it, 0], 120, 24, near(0, -1)),
            (cs.at[it, 3], 144, 16, near(1, 1)),
            (cs.at[it, 2], 160, 16, near(1, -1)),
            (cs.at[it, 1], 176, 16, near(-1, 1)),
            (cs.at[it, 0], 192, 16, near(-1, -1)),
        )
        for src, first, count, where in rims:
            pltpu.make_async_remote_copy(
                src, hr.at[it, first : first + count], send_sem.at[it, 0], recv_sem.at[it, 0],
                device_id=where,
            ).start()

        pl.when(it == 0)(prepare)

        wide = split(w[it])
        acc[...] = dot3((bm_h[:, 256:384], bm_l[:, 256:384]), wide)
        pltpu.make_async_remote_copy(
            hr.at[it, 0:208], hr.at[it, 0:208], send_sem.at[it, 0], recv_sem.at[it, 0],
            device_id=near(1, 0),
        ).wait_recv()
        wide = split(hr[it])
        acc[...] += dot3((bm_h[:, 0:256], bm_l[:, 0:256]), wide)

        place = lax.broadcasted_iota(jnp.int32, (1, 512), 1)

        def along_x(i, carry):
            rows = pl.ds(pl.multiple_of(i * 8, 8), 8)
            more = pl.ds(pl.multiple_of(128 + i * 8, 8), 8)
            mass, stiff = acc[rows, :], acc[more, :]
            total = jnp.zeros((8, 512), F32)
            for k in range(7):
                d = k - 3
                inside = (place + d >= 0) & (place + d < 512)
                kx = jnp.where(inside, xb[0, k : k + 1, :], 0.0)
                mx = jnp.where(inside, xb[1, k : k + 1, :], 0.0)
                if d:
                    a = pltpu.roll(mass, (512 - d) % 512, 1)
                    e = pltpu.roll(stiff, (512 - d) % 512, 1)
                else:
                    a, e = mass, stiff
                total = total + (kx * a + mx * e)
            r[rows, :] = b[rows, :] - c[rows, :] * total
            return carry

        lax.fori_loop(0, 16, along_x, 0)

        wide = split(r[...])
        for i in range(4):
            rows = slice(i * 128, i * 128 + 128)
            s[it, rows, :] = dot3((vxt_h[rows, :], vxt_l[rows, :]), wide, ((1,), (1,)))

        def send_group(src, dst, stage):
            def one(k, carry):
                g2 = (g + k) % 32
                pltpu.make_async_remote_copy(
                    src.at[it, pl.ds(pl.multiple_of(g2 * 16, 16), 16)],
                    dst.at[it, pl.ds(pl.multiple_of(g * 16, 16), 16)],
                    send_sem.at[it, stage], recv_sem.at[it, stage], device_id=group(g2),
                ).start()
                return carry

            lax.fori_loop(1, 32, one, 0)
            mine = pl.ds(pl.multiple_of(g * 16, 16), 16)
            dst[it, mine, :] = src[it, mine, :]

        def wait_group(dst, stage):
            part = dst.at[it, 0 : 31 * 16]
            pltpu.make_async_remote_copy(
                part, part, send_sem.at[it, stage], recv_sem.at[it, stage],
                device_id=group((g + 1) % 32),
            ).wait_recv()

        def send_ring(src, dst, stage):
            for k in RING:
                q2 = (q + k) % 16
                pltpu.make_async_remote_copy(
                    src.at[it, q2], dst.at[it, q],
                    send_sem.at[it, stage], recv_sem.at[it, stage], device_id=ring(q2),
                ).start()
            dst[it, q] = src[it, q]

        def wait_ring(dst, stage):
            part = dst.at[it, 0:15]
            pltpu.make_async_remote_copy(
                part, part, send_sem.at[it, stage], recv_sem.at[it, stage],
                device_id=ring((q + 1) % 16),
            ).wait_recv()

        send_group(s, ra, 1)
        wait_group(ra, 1)
        for k in range(16):
            sb[it, k] = ra[it, pl.ds(k, 32, stride=16), :]
        send_ring(sb, rb, 2)
        wait_ring(rb, 2)

        def gather(i, carry):
            h, y4 = i // 4, i % 4
            rows = pl.ds(pl.multiple_of(y4 * 8, 8), 8)
            for p in range(2):
                a = swap_blocks(rb[it, h * 4 + 2 * p, rows, :], sub, lane)
                e = swap_blocks(rb[it, h * 4 + 2 * p + 1, rows, :], sub, lane)
                low = jnp.where(lane < 64, a, pltpu.roll(e, 64, 1))
                high = jnp.where(lane < 64, pltpu.roll(a, 64, 1), e)
                cols = slice(p * 128, p * 128 + 128)
                m[pl.ds(pl.multiple_of(i * 16, 8), 8), cols] = low
                m[pl.ds(pl.multiple_of(i * 16 + 8, 8), 8), cols] = high
            return carry

        lax.fori_loop(0, 16, gather, 0)
        vzs = (vz_h[...], vz_l[...])
        m[...] = dot3(split(m[...]), vzs)
        m[...] = dot3((vyt_h[...], vyt_l[...]), split(m[...])) / den[...]
        m[...] = dot3((vy_h[...], vy_l[...]), split(m[...]))
        m[...] = dot3(split(m[...]), vzs, ((1,), (1,)))

        def scatter(i, carry):
            h, y4 = i // 4, i % 4
            rows = pl.ds(pl.multiple_of(y4 * 8, 8), 8)
            for p in range(2):
                cols = slice(p * 128, p * 128 + 128)
                low = m[pl.ds(pl.multiple_of(i * 16, 8), 8), cols]
                high = m[pl.ds(pl.multiple_of(i * 16 + 8, 8), 8), cols]
                a = jnp.where(lane < 64, low, pltpu.roll(high, 64, 1))
                e = jnp.where(lane < 64, pltpu.roll(low, 64, 1), high)
                mb[it, h * 4 + 2 * p, rows, :] = swap_blocks(a, sub, lane)
                mb[it, h * 4 + 2 * p + 1, rows, :] = swap_blocks(e, sub, lane)
            return carry

        lax.fori_loop(0, 16, scatter, 0)
        send_ring(mb, rb2, 3)
        wait_ring(rb2, 3)
        for k in range(16):
            for h in range(4):
                rows = rb2[it, k, h * 8 : h * 8 + 8, :]
                sa2[it, pl.ds(h * 128 + k, 8, stride=16), :] = rows
        send_group(sa2, ra2, 4)
        wait_group(ra2, 4)
        wide = split(jnp.transpose(ra2[it]))
        u[...] += dot3(wide, (vxt_h[...], vxt_l[...]))

        @pl.when(it + 1 < ITERS)
        def _():
            w[ITERS - 1] = c[...] * u[...]

        return carry

    lax.fori_loop(0, ITERS, step, 0)
    u_out[...] = u[...]
    r_out[...] = r[...]

    for it in range(ITERS):
        sent = hr.at[it, 0:208]
        pltpu.make_async_remote_copy(
            sent, sent, send_sem.at[it, 0], recv_sem.at[it, 0], device_id=near(1, 0)
        ).wait_send()
        for stage, part in ((1, s.at[it, 0:496]), (2, sb.at[it, 0:15]), (3, mb.at[it, 0:15]), (4, sa2.at[it, 0:496])):
            pltpu.make_async_remote_copy(
                part, part, send_sem.at[it, stage], recv_sem.at[it, stage], device_id=near(1, 0)
            ).wait_send()


def shards(solution, right_side, span_index, coef_table, xaxis_bands, yaxis_bands, zaxis_bands,
           xaxis_vectors, yaxis_vectors, zaxis_vectors, xaxis_values, yaxis_values, zaxis_values):
    flat = (128, 512)
    hbm = pl.BlockSpec(memory_space=pl.ANY)
    vmem = pl.BlockSpec(memory_space=pltpu.VMEM)
    smem = pl.BlockSpec(memory_space=pltpu.SMEM)
    V = pltpu.VMEM
    big = V((ITERS, 512, 128), F32)
    ring = V((ITERS, 16, 32, 128), F32)
    scratch = [
        V(flat, F32), V(flat, F32), V(flat, jnp.int32), V((512, 512), F32), V((256, 256), F32), V((256, 256), F32),
        V(flat, F32), V(flat, F32), V((ITERS, 2, 24, 512), F32), V((ITERS, 4, 16, 512), F32),
        V((ITERS, 256, 512), F32), V((ITERS, 128, 512), F32), V((256, 512), F32),
        big, big, ring, ring, V((256, 256), F32), ring, ring, big, big,
        V((256, 384), BF16), V((256, 384), BF16), V((512, 512), BF16), V((512, 512), BF16),
        V((256, 256), BF16), V((256, 256), BF16), V((256, 256), BF16), V((256, 256), BF16),
        V((256, 256), BF16), V((256, 256), BF16), V((256, 256), F32),
        pltpu.SemaphoreType.DMA((6,)), pltpu.SemaphoreType.DMA((ITERS, 5)), pltpu.SemaphoreType.DMA((ITERS, 5)),
    ]
    updated, residual = pl.pallas_call(
        kernel,
        out_shape=(jax.ShapeDtypeStruct(flat, F32), jax.ShapeDtypeStruct(flat, F32)),
        in_specs=[hbm, hbm, hbm, smem, vmem, smem, smem, hbm, hbm, hbm, vmem, vmem, vmem],
        out_specs=(vmem, vmem),
        scratch_shapes=scratch,
        compiler_params=pltpu.CompilerParams(collective_id=0, has_side_effects=True),
        name="richardson",
    )(
        solution.reshape(flat), right_side.reshape(flat), span_index.reshape(flat), coef_table,
        xaxis_bands, yaxis_bands, zaxis_bands, xaxis_vectors, yaxis_vectors, zaxis_vectors,
        xaxis_values.reshape(1, 512), yaxis_values.reshape(1, 256), zaxis_values.reshape(1, 256),
    )
    return updated.reshape(solution.shape), residual.reshape(solution.shape)


def solution(mesh):
    grid = P("py", "pz", None)
    return jax.shard_map(
        shards,
        mesh=mesh,
        in_specs=(grid, grid, grid, P(), P(), P(None, None, "py"), P(None, None, "pz"), P(), P(), P(), P(), P(), P()),
        out_specs=(grid, grid),
        check_vma=False,
    )
```

profile of v0, /device:TPU:1, one launch (start us, length us, event | category | flops | bytes accessed | tf_op | source)
XLA Modules:
  0.0 162.1 jit_solution(8627388018889753087)
XLA Ops:
  0.6 0.0 copy-start.2
  0.6 0.0 copy-start.1
  0.6 0.7 copy-done.2
  1.3 0.6 copy.16.yb
  1.9 1.3 copy.17.zb
  3.2 0.0 copy-done.1
  3.2 0.6 copy.15.xb
  3.8 155.8 %richardson.1 = (f32[128,512]{1,0:T(8,128)}, f32[128,512]{1,0:T(8,128)}) custom-call(f32[128,512]{1,0:T(8,128)} %bitcast.10, f32[128,512]{1,0:T(8,128)} %bitcast.11, s32[128,512]{1,0:T(8,128)} %bitcast.12, f32[8]{0:T(128)} %coef.1, f32[2,7,512]{2,1,0:T(8,128)} %copy.15.xb, f32[2,7,8]{2,1,0:T(8,128)} %copy.16.yb, f32[2,7,16]{2,1,0:T(8,128)} %copy.17.zb, ...), custom_call_target="tpu_custom_call" | custom-call | tf_op jit(solution)/shard_map/richardson/pallas_call | solution.py:393
  159.7 0.0 copy-start
  159.7 1.7 %copy.20 = f32[8,16,512]{2,1,0:T(8,128)} copy(f32[8,16,512]{2,1,0:T(8,128)} %bitcast.9) | data formatting | bytes 524288
  161.4 0.0 copy-done
  161.4 0.7 copy.21
Async XLA Ops:
  0.6 0.7 copy-start.2
  0.6 2.6 %copy-start.1 = (f32[2,7,512]{2,0,1:T(2,128)S(1)}, f32[2,7,512]{2,0,1:T(2,128)}, u32[]{:S(2)}) copy-start(f32[2,7,512]{2,0,1:T(2,128)} %param.17) | copy-start | bytes 86020
  159.7 1.7 %copy-start = (f32[128,512]{1,0:T(8,128)S(1)}, f32[128,512]{1,0:T(8,128)}, u32[]{:S(2)}) copy-start(f32[128,512]{1,0:T(8,128)} %get-tuple-element.5) | copy-start | bytes 786436
where the time goes:
time: 162 us
  Pallas kernels  156 us (96%)
  local copies, waits for them, and re-layouts  5.61 us (3%)
    pallas_call x1, Pallas kernels, shards(): pl.pallas_call(kernel, out_shape=(jax.ShapeDtypeStruct(flat, F32), jax.Sh...  156 us
    unnamed x11, local copies, waits for them, and re-layouts  5.61 us

commit v1 on v0

v1 whole, which is shorter than its diff:
```python
import jax
import jax.numpy as jnp
from jax import lax
from jax.experimental import pallas as pl
from jax.experimental.pallas import tpu as pltpu
from jax.sharding import PartitionSpec as P

ITERS = 2
F32 = jnp.float32
BF16 = jnp.bfloat16
RING = (8, 7, 9, 6, 10, 5, 11, 4, 12, 3, 13, 2, 14, 1, 15)


def split(v):
    hi = v.astype(BF16)
    return hi, (v - hi.astype(F32)).astype(BF16)


def dot3(a, b, dims=((1,), (0,))):
    def one(p, q):
        return lax.dot_general(p, q, (dims, ((), ())), preferred_element_type=F32)

    return one(a[0], b[0]) + one(a[0], b[1]) + one(a[1], b[0])


def swap_blocks(v, lane):
    v = pltpu.roll(v, 0, 1, stride=16, stride_axis=0)
    for bit in (1, 2, 4):
        v = jnp.where((lane // (16 * bit)) % 2 == 1, pltpu.roll(v, 8 - bit, 0), v)
    return pltpu.roll(v, 0, 1, stride=16, stride_axis=0)


def kernel(
    u_in, b_in, span_in, coef, xb_in, yb_in, zb_in, vx_in, vy_in, vz_in, xv_in, yv_in, zv_in,
    u_out, r_out,
    u, b, span, vx, vy, vz, xb, yb, zb, xv, yv, zv, c, r, zs, cs, hc, rl, hr, w, acc,
    s, ra, sb, rb, m, mb, rb2, sa2, ra2,
    bm_h, bm_l, vxt_h, vxt_l, vy_h, vy_l, vyt_h, vyt_l, vz_h, vz_l, den,
    kx_h, kx_l, mx_h, mx_l, load_sem, send_sem, recv_sem,
):
    py, pz = lax.axis_index("py"), lax.axis_index("pz")
    zh, yc = py // 8, py % 8
    x, zl = pz // 4, pz % 4
    g = yc * 4 + x
    q = zh * 4 + zl

    def device(py2, pz2):
        return {"py": py2, "pz": pz2}

    def group(g2):
        return device(zh * 8 + g2 // 4, (g2 % 4) * 4 + zl)

    def ring(q2):
        return device((q2 // 4) * 8 + yc, x * 4 + q2 % 4)

    def near(dy, dz):
        return device((py + 32 + dy) % 32, (pz + 16 + dz) % 16)

    loads = [
        pltpu.make_async_copy(src, dst, load_sem.at[i])
        for i, (src, dst) in enumerate(
            ((u_in, u), (span_in, span), (vx_in, vx), (vy_in, vy), (vz_in, vz), (b_in, b),
             (xb_in, xb), (yb_in, yb), (zb_in, zb), (xv_in, xv), (yv_in, yv), (zv_in, zv))
        )
    ]
    for load in loads:
        load.start()

    barrier = pltpu.get_barrier_semaphore()

    def greet(k, carry):
        pl.semaphore_signal(barrier, inc=1, device_id=group((g + k) % 32))
        return carry

    lax.fori_loop(1, 32, greet, 0)

    def greet_ring(k, carry):
        pl.semaphore_signal(barrier, inc=1, device_id=ring((q + k) % 16))
        return carry

    lax.fori_loop(1, 16, greet_ring, 0)
    sides = [(dy, dz) for dy in (-1, 0, 1) for dz in (-1, 0, 1) if dy or dz]
    for dy, dz in sides:
        pl.semaphore_signal(barrier, inc=1, device_id=near(dy, dz))
    top, bottom = yc == 7, yc == 0
    above, below = ((zh + 1) % 4) * 8, ((zh + 3) % 4) * 8

    @pl.when(bottom)
    def _():
        for k in range(3):
            pl.semaphore_signal(barrier, inc=1, device_id=device(below + 2 * k + 1, pz))

    @pl.when(top)
    def _():
        for k in range(1, 4):
            pl.semaphore_signal(barrier, inc=1, device_id=device(above + 2 * k, pz))

    cs[...] = jnp.zeros_like(cs)
    for it in range(ITERS):
        hr[it, pl.ds(144, 112), :] = jnp.zeros((112, 512), F32)

    loads[0].wait()
    loads[1].wait()

    def weigh(i, carry):
        rows = pl.ds(pl.multiple_of(i * 8, 8), 8)
        at = span[rows, :]
        v = jnp.full((8, 512), coef[0], F32)
        for e in range(1, 8):
            v = jnp.where(at == e, coef[e], v)
        c[rows, :] = v
        w[0, rows, :] = v * u[rows, :]
        return carry

    lax.fori_loop(0, 16, weigh, 0)
    pl.semaphore_wait(barrier, 31 + 15 + 8 + jnp.where(top | bottom, 0, 1))

    sub = lax.broadcasted_iota(jnp.int32, (8, 128), 0)
    lane = lax.broadcasted_iota(jnp.int32, (8, 128), 1)

    def prepare():
        def coords(tile):
            if tile == 2:
                return lane // 16, lane % 16
            col = lane + tile * 128
            yy = jnp.where(col < 48, col // 16 - 3, 8 + (col - 48) // 16)
            zz = col % 16
            k = col - 96
            edge = col >= 96
            yy = jnp.where(edge, k % 8, yy)
            zz = jnp.where(edge, jnp.where(k < 24, k // 8 - 3, 16 + (k - 24) // 8), zz)
            k = col - 144
            corner = k >= 0
            cc = k % 16
            y3 = jnp.where(cc >= 6, 2, jnp.where(cc >= 3, 1, 0))
            z3 = cc - 3 * y3
            t = k // 16
            yy = jnp.where(corner, jnp.where(t < 2, y3 - 3, 8 + y3), yy)
            zz = jnp.where(corner, jnp.where(t % 2 == 0, z3 - 3, 16 + z3), zz)
            bad = (corner & (cc >= 9)) | (col >= 208)
            gy, gz = py * 8 + yy, pz * 16 + zz
            bad = bad | (gy < 0) | (gy > 255) | (gz < 0) | (gz > 255)
            return jnp.where(bad, 1000, yy), jnp.where(bad, 1000, zz)

        for i in (6, 7, 8):
            loads[i].wait()
        pick = lax.broadcasted_iota(jnp.int32, (8, 16), 1) - lax.broadcasted_iota(jnp.int32, (8, 16), 0)
        columns = {
            (kind, k, half): jnp.sum(
                jnp.where(pick == half * 8, zb[k, kind : kind + 1, :], 0.0), axis=1, keepdims=True
            )
            for kind in range(2) for k in range(7) for half in range(2)
        }
        for tile in range(3):
            yy, zz = coords(tile)
            ez = {}
            for half in range(2):
                dz = zz - (half * 8 + sub) + 3
                for kind in range(2):
                    total = jnp.zeros((8, 128), F32)
                    for k in range(7):
                        total = jnp.where(dz == k, columns[kind, k, half], total)
                    ez[kind, half] = total
            for y in range(8):
                dy = yy - y + 3
                ey = []
                for kind in range(2):
                    total = jnp.zeros((8, 128), F32)
                    for k in range(7):
                        total = jnp.where(dy == k, yb[k, kind : kind + 1, y : y + 1], total)
                    ey.append(total)
                mass = [ey[1] * ez[1, half] for half in range(2)]
                stiff = [ey[0] * ez[1, half] + ey[1] * ez[0, half] for half in range(2)]
                for base, pair in ((0, mass), (128, stiff)):
                    hi, lo = split(jnp.concatenate(pair, axis=0))
                    at = slice(base + y * 16, base + y * 16 + 16)
                    bm_h[at, tile * 128 : tile * 128 + 128] = hi
                    bm_l[at, tile * 128 : tile * 128 + 128] = lo
        for kind, (big, small) in enumerate(((kx_h, kx_l), (mx_h, mx_l))):
            for i in range(4):
                for j in range(4):
                    at = (slice(j * 128, j * 128 + 128), slice(i * 128, i * 128 + 128))
                    if abs(i - j) > 1:
                        big[at] = jnp.zeros((128, 128), BF16)
                        small[at] = jnp.zeros((128, 128), BF16)
                        continue
                    for part in range(0, 128, 16):
                        shape = (16, 128)
                        k_of = (j - i) * 128 + part + 3 + lax.broadcasted_iota(jnp.int32, shape, 0)
                        k_of = k_of - lax.broadcasted_iota(jnp.int32, shape, 1)
                        total = jnp.zeros(shape, F32)
                        for k in range(7):
                            total = jnp.where(k_of == k, xb[k, kind : kind + 1, at[1]], total)
                        hi, lo = split(total)
                        big[j * 128 + part : j * 128 + part + 16, at[1]] = hi
                        small[j * 128 + part : j * 128 + part + 16, at[1]] = lo
        loads[2].wait()
        for i in range(4):
            cols = slice(i * 128, i * 128 + 128)
            hi, lo = split(jnp.transpose(vx[:, cols]))
            vxt_h[cols, :] = hi
            vxt_l[cols, :] = lo
        loads[3].wait()
        vy_h[...], vy_l[...] = split(vy[...])
        vyt_h[...], vyt_l[...] = split(jnp.transpose(vy[...]))
        loads[4].wait()
        for p in range(2):
            for e in range(2):
                for xx in range(4):
                    to = p * 128 + e * 64 + xx * 16
                    at = xx * 64 + (2 * p + e) * 16
                    hi, lo = split(vz[at : at + 16, :])
                    vz_h[to : to + 16, :] = hi
                    vz_l[to : to + 16, :] = lo
        for i in (9, 10, 11):
            loads[i].wait()
        column = jnp.transpose(jnp.broadcast_to(yv[...], (128, 256)))
        j = g * 16 + q
        row = lax.broadcasted_iota(jnp.int32, (1, 512), 1)
        mine = jnp.sum(jnp.where(row == j, xv[...], 0.0), axis=1, keepdims=True)
        for half in range(2):
            cols = slice(half * 128, half * 128 + 128)
            den[:, cols] = (column + zv[:, cols]) + mine
        loads[5].wait()

    def step(it, carry):
        for i in range(3):
            for side, first in enumerate((0, 13)):
                for t in range(4):
                    cols = slice(t * 128, t * 128 + 128)
                    full = w[it, :, cols].reshape(8, 16, 128)
                    zs[it, side, i * 8 : i * 8 + 8, cols] = full[:, first + i, :]
        for cy in range(2):
            for cz in range(2):
                for i in range(3):
                    row = (cy * 5 + i) * 16 + cz * 13
                    three = w[it, row : row + 3, :]
                    for t in range(4):
                        at = t * 9 + i * 3
                        cs[it, cy * 2 + cz, at : at + 3, :] = three[:, t * 128 : t * 128 + 128]
        own = w.at[it]

        def push(src, dst, stage, where, out=None):
            pltpu.make_async_remote_copy(
                src, dst, send_sem.at[it, stage if out is None else out], recv_sem.at[it, stage], device_id=where
            ).start()

        quarter = [slice(k * 128, k * 128 + 128) for k in range(4)]

        @pl.when(top)
        def _():
            for k in range(3):
                push(own.at[80:128, quarter[k]], rl.at[it], 5, device(zh * 8 + 2 * k + 1, pz))
            push(own.at[80:128, quarter[3]], hr.at[it, 0:48, quarter[3]], 0, near(1, 0), 5)

        @pl.when(bottom)
        def _():
            for k in range(1, 4):
                push(own.at[0:48, quarter[k]], rl.at[it], 5, device(zh * 8 + 2 * k, pz))
            push(own.at[0:48, quarter[0]], hr.at[it, 48:96, quarter[0]], 0, near(-1, 0), 5)

        push(cs.at[it, 3], hc.at[it, 0], 6, near(1, 1))
        push(cs.at[it, 2], hc.at[it, 1], 6, near(1, -1))
        push(cs.at[it, 1], hc.at[it, 2], 6, near(-1, 1))
        push(cs.at[it, 0], hc.at[it, 3], 6, near(-1, -1))

        @pl.when(jnp.logical_not(top))
        def _():
            push(own.at[80:128], hr.at[it, 0:48], 0, near(1, 0))

        @pl.when(jnp.logical_not(bottom))
        def _():
            push(own.at[0:48], hr.at[it, 48:96], 0, near(-1, 0))

        push(zs.at[it, 1], hr.at[it, 96:120], 0, near(0, 1))
        push(zs.at[it, 0], hr.at[it, 120:144], 0, near(0, -1))

        @pl.when(jnp.logical_not(top | bottom))
        def _():
            pltpu.make_async_remote_copy(
                rl.at[it], rl.at[it], send_sem.at[it, 5], recv_sem.at[it, 5], device_id=near(1, 0)
            ).wait_recv()
            odd = yc % 2 == 1
            first = pl.multiple_of(jnp.where(odd, 0, 48), 8)
            cols = pl.ds(pl.multiple_of((yc // 2) * 128, 128), 128)
            push(rl.at[it], hr.at[it, pl.ds(first, 48), cols], 0,
                 device(jnp.where(odd, above, below + 7), pz), 7)

        pl.when(it == 0)(prepare)

        wide = split(w[it])
        acc[...] = dot3((bm_h[:, 256:384], bm_l[:, 256:384]), wide)
        pltpu.make_async_remote_copy(
            hr.at[it, 0:144], hr.at[it, 0:144], send_sem.at[it, 0], recv_sem.at[it, 0],
            device_id=near(1, 0),
        ).wait_recv()
        pltpu.make_async_remote_copy(
            hc.at[it], hc.at[it], send_sem.at[it, 6], recv_sem.at[it, 6], device_id=near(1, 0)
        ).wait_recv()
        for corner in range(4):
            for t in range(4):
                at = 144 + corner * 16
                hr[it, at : at + 9, quarter[t]] = hc[it, corner, t * 9 : t * 9 + 9, :]
        wide = split(hr[it])
        acc[...] += dot3((bm_h[:, 0:256], bm_l[:, 0:256]), wide)

        total = dot3(split(acc[0:128, :]), (kx_h[...], kx_l[...]))
        total = total + dot3(split(acc[128:256, :]), (mx_h[...], mx_l[...]))
        r[...] = b[...] - c[...] * total

        @pl.when(it == ITERS - 1)
        def _():
            pltpu.make_async_copy(r, r_out, load_sem.at[12]).start()

        turned = [r[((8 - i) % 8) * 16 : ((8 - i) % 8) * 16 + 16, :] for i in range(8)]
        wide = split(jnp.concatenate(turned, axis=0))
        for i in range(4):
            rows = slice(i * 128, i * 128 + 128)
            s[it, rows, :] = dot3((vxt_h[rows, :], vxt_l[rows, :]), wide, ((1,), (1,)))

        def send_group(src, dst, stage, place=lambda g2: g2):
            def one(k, carry):
                g2 = (g + k) % 32
                pltpu.make_async_remote_copy(
                    src.at[it, pl.ds(pl.multiple_of(place(g2) * 16, 16), 16)],
                    dst.at[it, pl.ds(pl.multiple_of(g * 16, 16), 16)],
                    send_sem.at[it, stage], recv_sem.at[it, stage], device_id=group(g2),
                ).start()
                return carry

            lax.fori_loop(1, 32, one, 0)
            mine = pl.ds(pl.multiple_of(g * 16, 16), 16)
            dst[it, mine, :] = src[it, pl.ds(pl.multiple_of(place(g) * 16, 16), 16), :]

        def wait_group(dst, stage):
            part = dst.at[it, 0 : 31 * 16]
            pltpu.make_async_remote_copy(
                part, part, send_sem.at[it, stage], recv_sem.at[it, stage],
                device_id=group((g + 1) % 32),
            ).wait_recv()

        def send_ring(src, dst, stage):
            for k in RING:
                q2 = (q + k) % 16
                pltpu.make_async_remote_copy(
                    src.at[it, q2], dst.at[it, q],
                    send_sem.at[it, stage], recv_sem.at[it, stage], device_id=ring(q2),
                ).start()
            dst[it, q] = src[it, q]

        def wait_ring(dst, stage):
            part = dst.at[it, 0:15]
            pltpu.make_async_remote_copy(
                part, part, send_sem.at[it, stage], recv_sem.at[it, stage],
                device_id=ring((q + 1) % 16),
            ).wait_recv()

        send_group(s, ra, 1)
        wait_group(ra, 1)
        for k in range(16):
            sb[it, k] = ra[it, pl.ds(k, 32, stride=16), :]
        send_ring(sb, rb, 2)
        wait_ring(rb, 2)

        for i in range(16):
            h, y4 = i // 4, i % 4
            rows = slice(y4 * 8, y4 * 8 + 8)
            for p in range(2):
                a = swap_blocks(rb[it, h * 4 + 2 * p, rows, :], lane)
                e = swap_blocks(rb[it, h * 4 + 2 * p + 1, rows, :], lane)
                cols = quarter[p]
                m[i * 16 : i * 16 + 8, cols] = jnp.where(lane < 64, a, pltpu.roll(e, 64, 1))
                m[i * 16 + 8 : i * 16 + 16, cols] = jnp.where(lane < 64, pltpu.roll(a, 64, 1), e)
        vzs = (vz_h[...], vz_l[...])
        m[...] = dot3(split(m[...]), vzs)
        m[...] = dot3((vyt_h[...], vyt_l[...]), split(m[...])) / den[...]
        m[...] = dot3((vy_h[...], vy_l[...]), split(m[...]))
        m[...] = dot3(split(m[...]), vzs, ((1,), (1,)))

        for i in range(16):
            h, y4 = i // 4, i % 4
            rows = slice(y4 * 8, y4 * 8 + 8)
            for p in range(2):
                cols = quarter[p]
                low = m[i * 16 : i * 16 + 8, cols]
                high = m[i * 16 + 8 : i * 16 + 16, cols]
                a = jnp.where(lane < 64, low, pltpu.roll(high, 64, 1))
                e = jnp.where(lane < 64, pltpu.roll(low, 64, 1), high)
                mb[it, h * 4 + 2 * p, rows, :] = swap_blocks(a, lane)
                mb[it, h * 4 + 2 * p + 1, rows, :] = swap_blocks(e, lane)
        send_ring(mb, rb2, 3)
        wait_ring(rb2, 3)
        for k in range(16):
            for h in range(4):
                rows = rb2[it, k, h * 8 : h * 8 + 8, :]
                sa2[it, pl.ds(h * 128 + k, 8, stride=16), :] = rows
        send_group(sa2, ra2, 4, lambda g2: (g2 // 8) * 8 + (8 - g2 % 8) % 8)
        wait_group(ra2, 4)
        wide = split(jnp.transpose(ra2[it]))
        u[...] += dot3(wide, (vxt_h[...], vxt_l[...]))

        @pl.when(it + 1 < ITERS)
        def _():
            w[ITERS - 1] = c[...] * u[...]

        return carry

    lax.fori_loop(0, ITERS, step, 0)
    last = pltpu.make_async_copy(u, u_out, load_sem.at[13])
    last.start()
    for it in range(ITERS):
        @pl.when(jnp.logical_not(top | bottom))
        def _(it=it):
            pltpu.make_async_remote_copy(
                hr.at[it, 0:144], hr.at[it, 0:144], send_sem.at[it, 0], recv_sem.at[it, 0], device_id=near(1, 0)
            ).wait_send()
            pltpu.make_async_remote_copy(
                rl.at[it], rl.at[it], send_sem.at[it, 7], recv_sem.at[it, 0], device_id=near(1, 0)
            ).wait_send()

        @pl.when(top | bottom)
        def _(it=it):
            for stage, part in ((0, hr.at[it, 0:96]), (5, hr.at[it, 0:48])):
                pltpu.make_async_remote_copy(
                    part, part, send_sem.at[it, stage], recv_sem.at[it, stage], device_id=near(1, 0)
                ).wait_send()

        for stage, part in (
            (6, hc.at[it]),
            (1, s.at[it, 0:496]), (2, sb.at[it, 0:15]), (3, mb.at[it, 0:15]), (4, sa2.at[it, 0:496])):
            pltpu.make_async_remote_copy(
                part, part, send_sem.at[it, stage], recv_sem.at[it, stage], device_id=near(1, 0)
            ).wait_send()
    last.wait()
    pltpu.make_async_copy(r, r_out, load_sem.at[12]).wait()


def finish(u_in, r_in, u_out, r_out):
    u_out[...] = u_in[...]
    r_out[...] = r_in[...]


def shards(solution, right_side, span_index, coef_table, xaxis_bands, yaxis_bands, zaxis_bands,
           xaxis_vectors, yaxis_vectors, zaxis_vectors, xaxis_values, yaxis_values, zaxis_values):
    flat = (128, 512)
    hbm = pl.BlockSpec(memory_space=pl.ANY)
    vmem = pl.BlockSpec(memory_space=pltpu.VMEM)
    smem = pl.BlockSpec(memory_space=pltpu.SMEM)
    V = pltpu.VMEM
    big = V((ITERS, 512, 128), F32)
    ring = V((ITERS, 16, 32, 128), F32)
    scratch = [
        V(flat, F32), V(flat, F32), V(flat, jnp.int32), V((512, 512), F32), V((256, 256), F32), V((256, 256), F32),
        V((7, 2, 512), F32), V((7, 2, 8), F32), V((7, 2, 16), F32), V((1, 512), F32), V((1, 256), F32), V((1, 256), F32),
        V(flat, F32), V(flat, F32), V((ITERS, 2, 24, 512), F32), V((ITERS, 4, 40, 128), F32),
        V((ITERS, 4, 40, 128), F32), V((ITERS, 48, 128), F32),
        V((ITERS, 256, 512), F32), V((ITERS, 128, 512), F32), V((256, 512), F32),
        big, big, ring, ring, V((256, 256), F32), ring, ring, big, big,
        V((256, 384), BF16), V((256, 384), BF16), V((512, 512), BF16), V((512, 512), BF16),
        V((256, 256), BF16), V((256, 256), BF16), V((256, 256), BF16), V((256, 256), BF16),
        V((256, 256), BF16), V((256, 256), BF16), V((256, 256), F32),
        V((512, 512), BF16), V((512, 512), BF16), V((512, 512), BF16), V((512, 512), BF16),
        pltpu.SemaphoreType.DMA((14,)), pltpu.SemaphoreType.DMA((ITERS, 8)), pltpu.SemaphoreType.DMA((ITERS, 8)),
    ]
    updated, residual = pl.pallas_call(
        kernel,
        out_shape=(jax.ShapeDtypeStruct(flat, F32), jax.ShapeDtypeStruct(flat, F32)),
        in_specs=[hbm, hbm, hbm, smem] + [hbm] * 9,
        out_specs=(hbm, hbm),
        scratch_shapes=scratch,
        compiler_params=pltpu.CompilerParams(collective_id=0, has_side_effects=True),
        name="richardson",
    )(
        solution.reshape(flat), right_side.reshape(flat), span_index.reshape(flat), coef_table,
        jnp.swapaxes(xaxis_bands, 0, 1), jnp.swapaxes(yaxis_bands, 0, 1), jnp.swapaxes(zaxis_bands, 0, 1),
        xaxis_vectors, yaxis_vectors, zaxis_vectors,
        xaxis_values.reshape(1, 512), yaxis_values.reshape(1, 256), zaxis_values.reshape(1, 256),
    )
    updated, residual = pl.pallas_call(
        finish,
        out_shape=(jax.ShapeDtypeStruct(flat, F32), jax.ShapeDtypeStruct(flat, F32)),
        in_specs=[vmem, vmem],
        out_specs=(vmem, vmem),
        name="finish",
    )(updated, residual)
    return updated.reshape(solution.shape), residual.reshape(solution.shape)


def solution(mesh):
    grid = P("py", "pz", None)
    return jax.shard_map(
        shards,
        mesh=mesh,
        in_specs=(grid, grid, grid, P(), P(), P(None, None, "py"), P(None, None, "pz"), P(), P(), P(), P(), P(), P()),
        out_specs=(grid, grid),
        check_vma=False,
    )
```

time: 162 us -> 127 us (0.78)
  Pallas kernels: 156 us -> 126 us
  local copies, waits for them, and re-layouts: 5.61 us -> 0 us
    pallas_call x1, Pallas kernels: 156 us -> 124 us  [shards(): pl.pallas_call(kernel, out_shape=(jax.ShapeDtypeStruct(flat, F32), jax.Sh...]
    unnamed x11 -> x0, local copies, waits for them, and re-layouts: 5.61 us -> none
    pallas_call x0 -> x1, Pallas kernels: none -> 1.84 us  [shards(): pl.pallas_call(finish, out_shape=(jax.ShapeDtypeStruct(flat, F32), jax.Sh...]
where the time goes in v1:
time: 127 us
  Pallas kernels  126 us (99%)
    pallas_call x1, Pallas kernels, shards(): pl.pallas_call(kernel, out_shape=(jax.ShapeDtypeStruct(flat, F32), jax.Sh...  124 us

profile of v1, /device:TPU:1, one launch (start us, length us, event | category | flops | bytes accessed | tf_op | source)
XLA Modules:
  0.0 126.5 jit_solution(12672897654144488657)
XLA Ops:
  0.6 124.0 %richardson.1 = (f32[128,512]{1,0:T(8,128)}, f32[128,512]{1,0:T(8,128)}) custom-call(f32[128,512]{1,0:T(8,128)} %bitcast.11, f32[128,512]{1,0:T(8,128)} %bitcast.12, s32[128,512]{1,0:T(8,128)} %bitcast.13, f32[8]{0:T(128)} %coef.1, f32[7,2,512]{2,1,0:T(2,128)} %bitcast.14, f32[7,2,8]{2,1,0:T(2,128)} %bitcast.15, f32[7,2,16]{2,1,0:T(2,128)} %bitcast.16, ...), custom_call_target="tpu_custom_call" | custom-call | tf_op jit(solution)/shard_map/richardson/pallas_call | solution.py:465
  124.7 1.8 %finish.1 = (f32[128,512]{1,0:T(8,128)}, f32[128,512]{1,0:T(8,128)}) custom-call(f32[128,512]{1,0:T(8,128)} %get-tuple-element.6.u_in, f32[128,512]{1,0:T(8,128)} %get-tuple-element.7.r_in), custom_call_target="tpu_custom_call" | custom-call | tf_op jit(solution)/shard_map/finish/pallas_call | solution.py:479

commit v2 on v1

--- a/solution.py
+++ b/solution.py
@@ -8,6 +8,7 @@
 ITERS = 2
 F32 = jnp.float32
 BF16 = jnp.bfloat16
+PLACES = ((2, 3), (4, 5), (6, 1), (0, 7))
 RING = (8, 7, 9, 6, 10, 5, 11, 4, 12, 3, 13, 2, 14, 1, 15)
 
 
@@ -41,14 +42,19 @@
     py, pz = lax.axis_index("py"), lax.axis_index("pz")
     zh, yc = py // 8, py % 8
     x, zl = pz // 4, pz % 4
-    g = yc * 4 + x
+    top, bottom = yc == 7, yc == 0
+    edge = top | bottom
+    place = jnp.where(top, 7, jnp.where(bottom, 6, jnp.where(yc == 1, 5, yc - 2)))
+    g = place * 4 + x
     q = zh * 4 + zl
 
     def device(py2, pz2):
         return {"py": py2, "pz": pz2}
 
     def group(g2):
-        return device(zh * 8 + g2 // 4, (g2 % 4) * 4 + zl)
+        p = g2 // 4
+        yc2 = jnp.where(p == 7, 7, jnp.where(p == 6, 0, jnp.where(p == 5, 1, p + 2)))
+        return device(zh * 8 + yc2, (g2 % 4) * 4 + zl)
 
     def ring(q2):
         return device((q2 // 4) * 8 + yc, x * 4 + q2 % 4)
@@ -63,9 +69,8 @@
              (xb_in, xb), (yb_in, yb), (zb_in, zb), (xv_in, xv), (yv_in, yv), (zv_in, zv))
         )
     ]
-    for load in loads:
-        load.start()
-
+    loads[0].start()
+    loads[1].start()
     barrier = pltpu.get_barrier_semaphore()
 
     def greet(k, carry):
@@ -82,7 +87,6 @@
     sides = [(dy, dz) for dy in (-1, 0, 1) for dz in (-1, 0, 1) if dy or dz]
     for dy, dz in sides:
         pl.semaphore_signal(barrier, inc=1, device_id=near(dy, dz))
-    top, bottom = yc == 7, yc == 0
     above, below = ((zh + 1) % 4) * 8, ((zh + 3) % 4) * 8
 
     @pl.when(bottom)
@@ -95,6 +99,8 @@
         for k in range(1, 4):
             pl.semaphore_signal(barrier, inc=1, device_id=device(above + 2 * k, pz))
 
+    for load in loads[2:]:
+        load.start()
     cs[...] = jnp.zeros_like(cs)
     for it in range(ITERS):
         hr[it, pl.ds(144, 112), :] = jnp.zeros((112, 512), F32)
@@ -223,7 +229,14 @@
             den[:, cols] = (column + zv[:, cols]) + mine
         loads[5].wait()
 
-    def step(it, carry):
+    quarter = [slice(k * 128, k * 128 + 128) for k in range(4)]
+
+    def push(it, src, dst, stage, where, out=None):
+        pltpu.make_async_remote_copy(
+            src, dst, send_sem.at[it, stage if out is None else out], recv_sem.at[it, stage], device_id=where
+        ).start()
+
+    def rims(it):
         for i in range(3):
             for side, first in enumerate((0, 13)):
                 for t in range(4):
@@ -240,41 +253,35 @@
                         cs[it, cy * 2 + cz, at : at + 3, :] = three[:, t * 128 : t * 128 + 128]
         own = w.at[it]
 
-        def push(src, dst, stage, where, out=None):
-            pltpu.make_async_remote_copy(
-                src, dst, send_sem.at[it, stage if out is None else out], recv_sem.at[it, stage], device_id=where
-            ).start()
-
-        quarter = [slice(k * 128, k * 128 + 128) for k in range(4)]
-
         @pl.when(top)
         def _():
             for k in range(3):
-                push(own.at[80:128, quarter[k]], rl.at[it], 5, device(zh * 8 + 2 * k + 1, pz))
-            push(own.at[80:128, quarter[3]], hr.at[it, 0:48, quarter[3]], 0, near(1, 0), 5)
+                push(it, own.at[80:128, quarter[k]], rl.at[it], 5, device(zh * 8 + 2 * k + 1, pz))
+            push(it, own.at[80:128, quarter[3]], hr.at[it, 0:48, quarter[3]], 0, near(1, 0), 5)
 
         @pl.when(bottom)
         def _():
             for k in range(1, 4):
-                push(own.at[0:48, quarter[k]], rl.at[it], 5, device(zh * 8 + 2 * k, pz))
-            push(own.at[0:48, quarter[0]], hr.at[it, 48:96, quarter[0]], 0, near(-1, 0), 5)
-
-        push(cs.at[it, 3], hc.at[it, 0], 6, near(1, 1))
-        push(cs.at[it, 2], hc.at[it, 1], 6, near(1, -1))
-        push(cs.at[it, 1], hc.at[it, 2], 6, near(-1, 1))
-        push(cs.at[it, 0], hc.at[it, 3], 6, near(-1, -1))
+                push(it, own.at[0:48, quarter[k]], rl.at[it], 5, device(zh * 8 + 2 * k, pz))
+            push(it, own.at[0:48, quarter[0]], hr.at[it, 48:96, quarter[0]], 0, near(-1, 0), 5)
+
+        push(it, cs.at[it, 3], hc.at[it, 0], 6, near(1, 1))
+        push(it, cs.at[it, 2], hc.at[it, 1], 6, near(1, -1))
+        push(it, cs.at[it, 1], hc.at[it, 2], 6, near(-1, 1))
+        push(it, cs.at[it, 0], hc.at[it, 3], 6, near(-1, -1))
 
         @pl.when(jnp.logical_not(top))
         def _():
-            push(own.at[80:128], hr.at[it, 0:48], 0, near(1, 0))
+            push(it, own.at[80:128], hr.at[it, 0:48], 0, near(1, 0))
 
         @pl.when(jnp.logical_not(bottom))
         def _():
-            push(own.at[0:48], hr.at[it, 48:96], 0, near(-1, 0))
-
-        push(zs.at[it, 1], hr.at[it, 96:120], 0, near(0, 1))
-        push(zs.at[it, 0], hr.at[it, 120:144], 0, near(0, -1))
-
+            push(it, own.at[0:48], hr.at[it, 48:96], 0, near(-1, 0))
+
+        push(it, zs.at[it, 1], hr.at[it, 96:120], 0, near(0, 1))
+        push(it, zs.at[it, 0], hr.at[it, 120:144], 0, near(0, -1))
+
+    def relay(it):
         @pl.when(jnp.logical_not(top | bottom))
         def _():
             pltpu.make_async_remote_copy(
@@ -283,11 +290,14 @@
             odd = yc % 2 == 1
             first = pl.multiple_of(jnp.where(odd, 0, 48), 8)
             cols = pl.ds(pl.multiple_of((yc // 2) * 128, 128), 128)
-            push(rl.at[it], hr.at[it, pl.ds(first, 48), cols], 0,
+            push(it, rl.at[it], hr.at[it, pl.ds(first, 48), cols], 0,
                  device(jnp.where(odd, above, below + 7), pz), 7)
 
-        pl.when(it == 0)(prepare)
-
+    rims(0)
+    relay(0)
+    prepare()
+
+    def step(it, carry):
         wide = split(w[it])
         acc[...] = dot3((bm_h[:, 256:384], bm_l[:, 256:384]), wide)
         pltpu.make_async_remote_copy(
@@ -318,90 +328,100 @@
             rows = slice(i * 128, i * 128 + 128)
             s[it, rows, :] = dot3((vxt_h[rows, :], vxt_l[rows, :]), wide, ((1,), (1,)))
 
-        def send_group(src, dst, stage, place=lambda g2: g2):
-            def one(k, carry):
-                g2 = (g + k) % 32
-                pltpu.make_async_remote_copy(
-                    src.at[it, pl.ds(pl.multiple_of(place(g2) * 16, 16), 16)],
-                    dst.at[it, pl.ds(pl.multiple_of(g * 16, 16), 16)],
-                    send_sem.at[it, stage], recv_sem.at[it, stage], device_id=group(g2),
-                ).start()
-                return carry
-
-            lax.fori_loop(1, 32, one, 0)
-            mine = pl.ds(pl.multiple_of(g * 16, 16), 16)
-            dst[it, mine, :] = src[it, pl.ds(pl.multiple_of(place(g) * 16, 16), 16), :]
-
-        def wait_group(dst, stage):
-            part = dst.at[it, 0 : 31 * 16]
+        def wait_rows(part, stage):
             pltpu.make_async_remote_copy(
-                part, part, send_sem.at[it, stage], recv_sem.at[it, stage],
-                device_id=group((g + 1) % 32),
+                part, part, send_sem.at[it, 0], recv_sem.at[it, stage], device_id=near(1, 0)
             ).wait_recv()
 
-        def send_ring(src, dst, stage):
+        def send_ring(src, dst, rows, send, stage):
             for k in RING:
                 q2 = (q + k) % 16
                 pltpu.make_async_remote_copy(
-                    src.at[it, q2], dst.at[it, q],
-                    send_sem.at[it, stage], recv_sem.at[it, stage], device_id=ring(q2),
+                    src.at[it, q2, rows], dst.at[it, q, rows],
+                    send_sem.at[it, send], recv_sem.at[it, stage], device_id=ring(q2),
                 ).start()
-            dst[it, q] = src[it, q]
-
-        def wait_ring(dst, stage):
-            part = dst.at[it, 0:15]
+            dst[it, q, rows] = src[it, q, rows]
+
+        def block(i):
+            return pl.ds(pl.multiple_of(i * 16, 16), 16)
+
+        def send_block(k, carry):
+            g2 = (g + k) % 32
             pltpu.make_async_remote_copy(
-                part, part, send_sem.at[it, stage], recv_sem.at[it, stage],
-                device_id=ring((q + 1) % 16),
-            ).wait_recv()
-
-        send_group(s, ra, 1)
-        wait_group(ra, 1)
+                s.at[it, block(g2)], ra.at[it, block(g)],
+                send_sem.at[it, 1], recv_sem.at[it, jnp.where(edge, 8, 1)], device_id=group(g2),
+            ).start()
+            return carry
+
+        lax.fori_loop(1, 32, send_block, 0)
+        ra[it, block(g), :] = s[it, block(g), :]
+        pl.when(edge)(lambda: wait_rows(ra.at[it, 0 : 24 * 16], 1))
+        pl.when(jnp.logical_not(edge))(lambda: wait_rows(ra.at[it, 0 : 23 * 16], 1))
         for k in range(16):
-            sb[it, k] = ra[it, pl.ds(k, 32, stride=16), :]
-        send_ring(sb, rb, 2)
-        wait_ring(rb, 2)
-
-        for i in range(16):
-            h, y4 = i // 4, i % 4
-            rows = slice(y4 * 8, y4 * 8 + 8)
-            for p in range(2):
-                a = swap_blocks(rb[it, h * 4 + 2 * p, rows, :], lane)
-                e = swap_blocks(rb[it, h * 4 + 2 * p + 1, rows, :], lane)
-                cols = quarter[p]
-                m[i * 16 : i * 16 + 8, cols] = jnp.where(lane < 64, a, pltpu.roll(e, 64, 1))
-                m[i * 16 + 8 : i * 16 + 16, cols] = jnp.where(lane < 64, pltpu.roll(a, 64, 1), e)
+            sb[it, k, 0:24] = ra[it, pl.ds(k, 24, stride=16), :]
+        send_ring(sb, rb, slice(0, 24), 2, 2)
+        pl.when(edge)(lambda: wait_rows(ra.at[it, 0 : 7 * 16], 8))
+        pl.when(jnp.logical_not(edge))(lambda: wait_rows(ra.at[it, 0 : 8 * 16], 8))
+        for k in range(16):
+            sb[it, k, 24:32] = ra[it, pl.ds(24 * 16 + k, 8, stride=16), :]
+        send_ring(sb, rb, slice(24, 32), 2, 2)
+        wait_rows(rb.at[it, 0:15], 2)
+
+        for h in range(4):
+            for t in range(4):
+                rows = slice(t * 8, t * 8 + 8)
+                one, two = ((h * 8 + yy) * 8 for yy in PLACES[t])
+                for p in range(2):
+                    a = swap_blocks(rb[it, h * 4 + 2 * p, rows, :], lane)
+                    e = swap_blocks(rb[it, h * 4 + 2 * p + 1, rows, :], lane)
+                    m[one : one + 8, quarter[p]] = jnp.where(lane < 64, a, pltpu.roll(e, 64, 1))
+                    m[two : two + 8, quarter[p]] = jnp.where(lane < 64, pltpu.roll(a, 64, 1), e)
         vzs = (vz_h[...], vz_l[...])
         m[...] = dot3(split(m[...]), vzs)
         m[...] = dot3((vyt_h[...], vyt_l[...]), split(m[...])) / den[...]
         m[...] = dot3((vy_h[...], vy_l[...]), split(m[...]))
         m[...] = dot3(split(m[...]), vzs, ((1,), (1,)))
 
-        for i in range(16):
-            h, y4 = i // 4, i % 4
-            rows = slice(y4 * 8, y4 * 8 + 8)
-            for p in range(2):
-                cols = quarter[p]
-                low = m[i * 16 : i * 16 + 8, cols]
-                high = m[i * 16 + 8 : i * 16 + 16, cols]
-                a = jnp.where(lane < 64, low, pltpu.roll(high, 64, 1))
-                e = jnp.where(lane < 64, pltpu.roll(low, 64, 1), high)
-                mb[it, h * 4 + 2 * p, rows, :] = swap_blocks(a, lane)
-                mb[it, h * 4 + 2 * p + 1, rows, :] = swap_blocks(e, lane)
-        send_ring(mb, rb2, 3)
-        wait_ring(rb2, 3)
-        for k in range(16):
+        for t in (3, 0, 1, 2):
+            rows = slice(t * 8, t * 8 + 8)
             for h in range(4):
-                rows = rb2[it, k, h * 8 : h * 8 + 8, :]
-                sa2[it, pl.ds(h * 128 + k, 8, stride=16), :] = rows
-        send_group(sa2, ra2, 4, lambda g2: (g2 // 8) * 8 + (8 - g2 % 8) % 8)
-        wait_group(ra2, 4)
+                one, two = ((h * 8 + yy) * 8 for yy in PLACES[t])
+                for p in range(2):
+                    low, high = m[one : one + 8, quarter[p]], m[two : two + 8, quarter[p]]
+                    a = jnp.where(lane < 64, low, pltpu.roll(high, 64, 1))
+                    e = jnp.where(lane < 64, pltpu.roll(low, 64, 1), high)
+                    mb[it, h * 4 + 2 * p, rows, :] = swap_blocks(a, lane)
+                    mb[it, h * 4 + 2 * p + 1, rows, :] = swap_blocks(e, lane)
+            send_ring(mb, rb2, rows, 3, 9 + t)
+        for t in (3, 0, 1, 2):
+            wait_rows(rb2.at[it, 0:15, 0:8], 9 + t)
+            for k in range(16):
+                sa2[it, pl.ds(t * 128 + k, 8, stride=16), :] = rb2[it, k, t * 8 : t * 8 + 8, :]
+            for i in range(8):
+                row = (g + i) % 8
+                g2 = t * 8 + row
+                src = block(t * 8 + (8 - row) % 8)
+
+                @pl.when(g2 != g)
+                def _(g2=g2, src=src):
+                    pltpu.make_async_remote_copy(
+                        sa2.at[it, src], ra2.at[it, block(g)],
+                        send_sem.at[it, 4], recv_sem.at[it, 4], device_id=group(g2),
+                    ).start()
+
+                @pl.when(g2 == g)
+                def _(src=src):
+                    ra2[it, block(g), :] = sa2[it, src, :]
+
+        pl.when(it + 1 < ITERS)(lambda: relay(it + 1))
+        wait_rows(ra2.at[it, 0 : 31 * 16], 4)
         wide = split(jnp.transpose(ra2[it]))
         u[...] += dot3(wide, (vxt_h[...], vxt_l[...]))
 
         @pl.when(it + 1 < ITERS)
         def _():
-            w[ITERS - 1] = c[...] * u[...]
+            w[it + 1] = c[...] * u[...]
+            rims(it + 1)
 
         return carry
 
@@ -460,7 +480,7 @@
         V((256, 256), BF16), V((256, 256), BF16), V((256, 256), BF16), V((256, 256), BF16),
         V((256, 256), BF16), V((256, 256), BF16), V((256, 256), F32),
         V((512, 512), BF16), V((512, 512), BF16), V((512, 512), BF16), V((512, 512), BF16),
-        pltpu.SemaphoreType.DMA((14,)), pltpu.SemaphoreType.DMA((ITERS, 8)), pltpu.SemaphoreType.DMA((ITERS, 8)),
+        pltpu.SemaphoreType.DMA((14,)), pltpu.SemaphoreType.DMA((ITERS, 8)), pltpu.SemaphoreType.DMA((ITERS, 13)),
     ]
     updated, residual = pl.pallas_call(
         kernel,

time: 127 us -> 127 us (level)
  no operation moved by 1% of the time
where the time goes in v2:
time: 127 us
  Pallas kernels  126 us (99%)
    pallas_call x1, Pallas kernels, shards(): pl.pallas_call(kernel, out_shape=(jax.ShapeDtypeStruct(flat, F32), jax.Sh...  125 us

profile of v2, /device:TPU:1, one launch (start us, length us, event | category | flops | bytes accessed | tf_op | source)
XLA Modules:
  0.0 127.1 jit_solution(14808715378639436291)
XLA Ops:
  0.6 124.6 %richardson.1 = (f32[128,512]{1,0:T(8,128)}, f32[128,512]{1,0:T(8,128)}) custom-call(f32[128,512]{1,0:T(8,128)} %bitcast.11, f32[128,512]{1,0:T(8,128)} %bitcast.12, s32[128,512]{1,0:T(8,128)} %bitcast.13, f32[8]{0:T(128)} %coef.1, f32[7,2,512]{2,1,0:T(2,128)} %bitcast.14, f32[7,2,8]{2,1,0:T(2,128)} %bitcast.15, f32[7,2,16]{2,1,0:T(2,128)} %bitcast.16, ...), custom_call_target="tpu_custom_call" | custom-call | tf_op jit(solution)/shard_map/richardson/pallas_call | solution.py:485
  125.3 1.8 %finish.1 = (f32[128,512]{1,0:T(8,128)}, f32[128,512]{1,0:T(8,128)}) custom-call(f32[128,512]{1,0:T(8,128)} %get-tuple-element.6.u_in, f32[128,512]{1,0:T(8,128)} %get-tuple-element.7.r_in), custom_call_target="tpu_custom_call" | custom-call | tf_op jit(solution)/shard_map/finish/pallas_call | solution.py:499

commit v3 on v2

--- a/solution.py
+++ b/solution.py
@@ -8,7 +8,7 @@
 ITERS = 2
 F32 = jnp.float32
 BF16 = jnp.bfloat16
-PLACES = ((2, 3), (4, 5), (6, 1), (0, 7))
+PLACES = ((0, 1), (2, 3), (4, 5), (6, 7))
 RING = (8, 7, 9, 6, 10, 5, 11, 4, 12, 3, 13, 2, 14, 1, 15)
 
 
@@ -35,7 +35,7 @@
     u_in, b_in, span_in, coef, xb_in, yb_in, zb_in, vx_in, vy_in, vz_in, xv_in, yv_in, zv_in,
     u_out, r_out,
     u, b, span, vx, vy, vz, xb, yb, zb, xv, yv, zv, c, r, zs, cs, hc, rl, hr, w, acc,
-    s, ra, sb, rb, m, mb, rb2, sa2, ra2,
+    s, ra, sb, rb, rc, se, rd, m, mb, rb2, sa2, rm, sn, ra2,
     bm_h, bm_l, vxt_h, vxt_l, vy_h, vy_l, vyt_h, vyt_l, vz_h, vz_l, den,
     kx_h, kx_l, mx_h, mx_l, load_sem, send_sem, recv_sem,
 ):
@@ -44,17 +44,17 @@
     x, zl = pz // 4, pz % 4
     top, bottom = yc == 7, yc == 0
     edge = top | bottom
-    place = jnp.where(top, 7, jnp.where(bottom, 6, jnp.where(yc == 1, 5, yc - 2)))
-    g = place * 4 + x
+    core = yc % 2
+    first, second = core == 0, core == 1
+    g = yc * 4 + x
+    mine = (yc // 2) * 4 + x
     q = zh * 4 + zl
 
     def device(py2, pz2):
         return {"py": py2, "pz": pz2}
 
     def group(g2):
-        p = g2 // 4
-        yc2 = jnp.where(p == 7, 7, jnp.where(p == 6, 0, jnp.where(p == 5, 1, p + 2)))
-        return device(zh * 8 + yc2, (g2 % 4) * 4 + zl)
+        return device(zh * 8 + g2 // 4, (g2 % 4) * 4 + zl)
 
     def ring(q2):
         return device((q2 // 4) * 8 + yc, x * 4 + q2 % 4)
@@ -221,12 +221,12 @@
         for i in (9, 10, 11):
             loads[i].wait()
         column = jnp.transpose(jnp.broadcast_to(yv[...], (128, 256)))
-        j = g * 16 + q
+        j = jnp.where(first, mine * 16 + q, 256 + q * 16 + mine)
         row = lax.broadcasted_iota(jnp.int32, (1, 512), 1)
-        mine = jnp.sum(jnp.where(row == j, xv[...], 0.0), axis=1, keepdims=True)
+        shift = jnp.sum(jnp.where(row == j, xv[...], 0.0), axis=1, keepdims=True)
         for half in range(2):
             cols = slice(half * 128, half * 128 + 128)
-            den[:, cols] = (column + zv[:, cols]) + mine
+            den[:, cols] = (column + zv[:, cols]) + shift
         loads[5].wait()
 
     quarter = [slice(k * 128, k * 128 + 128) for k in range(4)]
@@ -288,9 +288,9 @@
                 rl.at[it], rl.at[it], send_sem.at[it, 5], recv_sem.at[it, 5], device_id=near(1, 0)
             ).wait_recv()
             odd = yc % 2 == 1
-            first = pl.multiple_of(jnp.where(odd, 0, 48), 8)
+            start = pl.multiple_of(jnp.where(odd, 0, 48), 8)
             cols = pl.ds(pl.multiple_of((yc // 2) * 128, 128), 128)
-            push(it, rl.at[it], hr.at[it, pl.ds(first, 48), cols], 0,
+            push(it, rl.at[it], hr.at[it, pl.ds(start, 48), cols], 0,
                  device(jnp.where(odd, above, below + 7), pz), 7)
 
     rims(0)
@@ -324,7 +324,10 @@
 
         turned = [r[((8 - i) % 8) * 16 : ((8 - i) % 8) * 16 + 16, :] for i in range(8)]
         wide = split(jnp.concatenate(turned, axis=0))
-        for i in range(4):
+        def block(i):
+            return pl.ds(pl.multiple_of(i * 16, 16), 16)
+
+        def modes(i):
             rows = slice(i * 128, i * 128 + 128)
             s[it, rows, :] = dot3((vxt_h[rows, :], vxt_l[rows, :]), wide, ((1,), (1,)))
 
@@ -333,39 +336,62 @@
                 part, part, send_sem.at[it, 0], recv_sem.at[it, stage], device_id=near(1, 0)
             ).wait_recv()
 
-        def send_ring(src, dst, rows, send, stage):
+        modes(2)
+        modes(3)
+        for k in RING:
+            q2 = (q + k) % 16
+            push(it, s.at[it, block(16 + q2)], rc.at[it, block(q)], 2, ring(q2))
+        rc[it, block(q), :] = s[it, block(16 + q), :]
+        modes(0)
+        modes(1)
+
+        def send_some(src, dst, stage, where, count, own, source=lambda i: i):
+            def one(k, carry):
+                i = (mine + k) % count if count == 16 else (g + k) % 32
+
+                @pl.when(i != own)
+                def _():
+                    push(it, src.at[it, block(source(i))], dst, stage, where(i))
+
+                return carry
+
+            lax.fori_loop(0, count, one, 0)
+
+        def first_core(i):
+            return device(zh * 8 + (i // 4) * 2, (i % 4) * 4 + zl)
+
+        def second_core(i):
+            return device(zh * 8 + (i // 4) * 2 + 1, (i % 4) * 4 + zl)
+
+        none = 99
+        send_some(s, ra.at[it, block(g)], 1, first_core, 16, jnp.where(first, mine, none))
+
+        @pl.when(first)
+        def _():
+            ra[it, block(g), :] = s[it, block(mine), :]
+            wait_rows(ra.at[it, 0 : 31 * 16], 1)
+            for k in range(16):
+                sb[it, k] = ra[it, pl.ds(k, 32, stride=16), :]
             for k in RING:
                 q2 = (q + k) % 16
-                pltpu.make_async_remote_copy(
-                    src.at[it, q2, rows], dst.at[it, q, rows],
-                    send_sem.at[it, send], recv_sem.at[it, stage], device_id=ring(q2),
-                ).start()
-            dst[it, q, rows] = src[it, q, rows]
-
-        def block(i):
-            return pl.ds(pl.multiple_of(i * 16, 16), 16)
-
-        def send_block(k, carry):
-            g2 = (g + k) % 32
-            pltpu.make_async_remote_copy(
-                s.at[it, block(g2)], ra.at[it, block(g)],
-                send_sem.at[it, 1], recv_sem.at[it, jnp.where(edge, 8, 1)], device_id=group(g2),
-            ).start()
-            return carry
-
-        lax.fori_loop(1, 32, send_block, 0)
-        ra[it, block(g), :] = s[it, block(g), :]
-        pl.when(edge)(lambda: wait_rows(ra.at[it, 0 : 24 * 16], 1))
-        pl.when(jnp.logical_not(edge))(lambda: wait_rows(ra.at[it, 0 : 23 * 16], 1))
+                push(it, sb.at[it, q2], rb.at[it, q], 3, ring(q2))
+            rb[it, q] = sb[it, q]
+
+        wait_rows(rc.at[it, 0 : 15 * 16], 2)
         for k in range(16):
-            sb[it, k, 0:24] = ra[it, pl.ds(k, 24, stride=16), :]
-        send_ring(sb, rb, slice(0, 24), 2, 2)
-        pl.when(edge)(lambda: wait_rows(ra.at[it, 0 : 7 * 16], 8))
-        pl.when(jnp.logical_not(edge))(lambda: wait_rows(ra.at[it, 0 : 8 * 16], 8))
-        for k in range(16):
-            sb[it, k, 24:32] = ra[it, pl.ds(24 * 16 + k, 8, stride=16), :]
-        send_ring(sb, rb, slice(24, 32), 2, 2)
-        wait_rows(rb.at[it, 0:15], 2)
+            se[it, k * 16 : k * 16 + 16, :] = rc[it, pl.ds(k, 16, stride=16), :]
+        send_some(se, rd.at[it, block(g)], 4, second_core, 16, jnp.where(second, mine, none))
+
+        @pl.when(first)
+        def _():
+            wait_rows(rb.at[it, 0:15], 3)
+
+        @pl.when(second)
+        def _():
+            rd[it, block(g), :] = se[it, block(mine), :]
+            wait_rows(rd.at[it, 0 : 31 * 16], 4)
+            for k in range(16):
+                rb[it, k] = rd[it, pl.ds(k, 32, stride=16), :]
 
         for h in range(4):
             for t in range(4):
@@ -382,7 +408,7 @@
         m[...] = dot3((vy_h[...], vy_l[...]), split(m[...]))
         m[...] = dot3(split(m[...]), vzs, ((1,), (1,)))
 
-        for t in (3, 0, 1, 2):
+        for t in range(4):
             rows = slice(t * 8, t * 8 + 8)
             for h in range(4):
                 one, two = ((h * 8 + yy) * 8 for yy in PLACES[t])
@@ -392,29 +418,53 @@
                     e = jnp.where(lane < 64, pltpu.roll(low, 64, 1), high)
                     mb[it, h * 4 + 2 * p, rows, :] = swap_blocks(a, lane)
                     mb[it, h * 4 + 2 * p + 1, rows, :] = swap_blocks(e, lane)
-            send_ring(mb, rb2, rows, 3, 9 + t)
-        for t in (3, 0, 1, 2):
-            wait_rows(rb2.at[it, 0:15, 0:8], 9 + t)
+
+        def turn(i):
+            return (i // 8) * 8 + (8 - i % 8) % 8
+
+        def by_group(src, dst):
             for k in range(16):
-                sa2[it, pl.ds(t * 128 + k, 8, stride=16), :] = rb2[it, k, t * 8 : t * 8 + 8, :]
-            for i in range(8):
-                row = (g + i) % 8
-                g2 = t * 8 + row
-                src = block(t * 8 + (8 - row) % 8)
-
-                @pl.when(g2 != g)
-                def _(g2=g2, src=src):
-                    pltpu.make_async_remote_copy(
-                        sa2.at[it, src], ra2.at[it, block(g)],
-                        send_sem.at[it, 4], recv_sem.at[it, 4], device_id=group(g2),
-                    ).start()
-
-                @pl.when(g2 == g)
-                def _(src=src):
-                    ra2[it, block(g), :] = sa2[it, src, :]
-
-        pl.when(it + 1 < ITERS)(lambda: relay(it + 1))
-        wait_rows(ra2.at[it, 0 : 31 * 16], 4)
+                for h in range(4):
+                    dst[it, pl.ds(h * 128 + k, 8, stride=16), :] = src[it, k, h * 8 : h * 8 + 8, :]
+
+        @pl.when(first)
+        def _():
+            for k in RING:
+                q2 = (q + k) % 16
+                push(it, mb.at[it, q2], rb2.at[it, q], 8, ring(q2))
+            rb2[it, q] = mb[it, q]
+
+        @pl.when(second)
+        def _():
+            by_group(mb, sa2)
+            send_some(sa2, rm.at[it, block(mine)], 10, group, 32, g, turn)
+            rm[it, block(mine), :] = sa2[it, block(turn(g)), :]
+            wait_rows(rm.at[it, 0 : 15 * 16], 10)
+
+        @pl.when(first)
+        def _():
+            wait_rows(rm.at[it, 0 : 16 * 16], 10)
+
+        for k in range(16):
+            sn[it, k * 16 : k * 16 + 16, :] = rm[it, pl.ds(k, 16, stride=16), :]
+        for k in RING:
+            q2 = (q + k) % 16
+            push(it, sn.at[it, block(q2)], ra2.at[it, block(16 + q)], 11, ring(q2))
+        ra2[it, block(16 + q), :] = sn[it, block(q), :]
+
+        @pl.when(first)
+        def _():
+            wait_rows(rb2.at[it, 0:15], 8)
+            by_group(rb2, sa2)
+            send_some(sa2, ra2.at[it, block(mine)], 9, group, 32, g, turn)
+            ra2[it, block(mine), :] = sa2[it, block(turn(g)), :]
+            wait_rows(ra2.at[it, 0 : 15 * 16], 9)
+
+        @pl.when(second)
+        def _():
+            wait_rows(ra2.at[it, 0 : 16 * 16], 9)
+
+        wait_rows(ra2.at[it, 0 : 15 * 16], 11)
         wide = split(jnp.transpose(ra2[it]))
         u[...] += dot3(wide, (vxt_h[...], vxt_l[...]))
 
@@ -422,6 +472,7 @@
         def _():
             w[it + 1] = c[...] * u[...]
             rims(it + 1)
+            relay(it + 1)
 
         return carry
 
@@ -445,12 +496,29 @@
                     part, part, send_sem.at[it, stage], recv_sem.at[it, stage], device_id=near(1, 0)
                 ).wait_send()
 
-        for stage, part in (
-            (6, hc.at[it]),
-            (1, s.at[it, 0:496]), (2, sb.at[it, 0:15]), (3, mb.at[it, 0:15]), (4, sa2.at[it, 0:496])):
+        def sent(stage, part, it=it):
             pltpu.make_async_remote_copy(
                 part, part, send_sem.at[it, stage], recv_sem.at[it, stage], device_id=near(1, 0)
             ).wait_send()
+
+        sent(6, hc.at[it])
+        sent(2, ra.at[it, 0 : 15 * 16])
+        sent(11, ra.at[it, 0 : 15 * 16])
+
+        @pl.when(first)
+        def _(it=it, sent=sent):
+            sent(1, ra.at[it, 0 : 15 * 16])
+            sent(3, sb.at[it, 0:15])
+            sent(4, ra.at[it, 0 : 16 * 16])
+            sent(8, sb.at[it, 0:15])
+            sent(9, ra.at[it, 0 : 31 * 16])
+
+        @pl.when(second)
+        def _(it=it, sent=sent):
+            sent(1, ra.at[it, 0 : 16 * 16])
+            sent(4, ra.at[it, 0 : 15 * 16])
+            sent(10, ra.at[it, 0 : 31 * 16])
+
     last.wait()
     pltpu.make_async_copy(r, r_out, load_sem.at[12]).wait()
 
@@ -468,6 +536,7 @@
     smem = pl.BlockSpec(memory_space=pltpu.SMEM)
     V = pltpu.VMEM
     big = V((ITERS, 512, 128), F32)
+    half = V((ITERS, 256, 128), F32)
     ring = V((ITERS, 16, 32, 128), F32)
     scratch = [
         V(flat, F32), V(flat, F32), V(flat, jnp.int32), V((512, 512), F32), V((256, 256), F32), V((256, 256), F32),
@@ -475,12 +544,12 @@
         V(flat, F32), V(flat, F32), V((ITERS, 2, 24, 512), F32), V((ITERS, 4, 40, 128), F32),
         V((ITERS, 4, 40, 128), F32), V((ITERS, 48, 128), F32),
         V((ITERS, 256, 512), F32), V((ITERS, 128, 512), F32), V((256, 512), F32),
-        big, big, ring, ring, V((256, 256), F32), ring, ring, big, big,
+        big, big, ring, ring, half, half, big, V((256, 256), F32), ring, ring, big, half, half, big,
         V((256, 384), BF16), V((256, 384), BF16), V((512, 512), BF16), V((512, 512), BF16),
         V((256, 256), BF16), V((256, 256), BF16), V((256, 256), BF16), V((256, 256), BF16),
         V((256, 256), BF16), V((256, 256), BF16), V((256, 256), F32),
         V((512, 512), BF16), V((512, 512), BF16), V((512, 512), BF16), V((512, 512), BF16),
-        pltpu.SemaphoreType.DMA((14,)), pltpu.SemaphoreType.DMA((ITERS, 8)), pltpu.SemaphoreType.DMA((ITERS, 13)),
+        pltpu.SemaphoreType.DMA((14,)), pltpu.SemaphoreType.DMA((ITERS, 12)), pltpu.SemaphoreType.DMA((ITERS, 12)),
     ]
     updated, residual = pl.pallas_call(
         kernel,

time: 127 us -> 115 us (0.906)
  Pallas kernels: 126 us -> 114 us
    pallas_call x1, Pallas kernels: 125 us -> 113 us  [shards(): pl.pallas_call(kernel, out_shape=(jax.ShapeDtypeStruct(flat, F32), jax.Sh...]
where the time goes in v3:
time: 115 us
  Pallas kernels  114 us (99%)
    pallas_call x1, Pallas kernels, shards(): pl.pallas_call(kernel, out_shape=(jax.ShapeDtypeStruct(flat, F32), jax.Sh...  113 us

profile of v3, /device:TPU:1, one launch (start us, length us, event | category | flops | bytes accessed | tf_op | source)
XLA Modules:
  0.0 115.0 jit_solution(15044231761945362771)
XLA Ops:
  0.6 112.6 %richardson.1 = (f32[128,512]{1,0:T(8,128)}, f32[128,512]{1,0:T(8,128)}) custom-call(f32[128,512]{1,0:T(8,128)} %bitcast.11, f32[128,512]{1,0:T(8,128)} %bitcast.12, s32[128,512]{1,0:T(8,128)} %bitcast.13, f32[8]{0:T(128)} %coef.1, f32[7,2,512]{2,1,0:T(2,128)} %bitcast.14, f32[7,2,8]{2,1,0:T(2,128)} %bitcast.15, f32[7,2,16]{2,1,0:T(2,128)} %bitcast.16, ...), custom_call_target="tpu_custom_call" | custom-call | tf_op jit(solution)/shard_map/richardson/pallas_call | solution.py:554
  113.2 1.8 %finish.1 = (f32[128,512]{1,0:T(8,128)}, f32[128,512]{1,0:T(8,128)}) custom-call(f32[128,512]{1,0:T(8,128)} %get-tuple-element.6.u_in, f32[128,512]{1,0:T(8,128)} %get-tuple-element.7.r_in), custom_call_target="tpu_custom_call" | custom-call | tf_op jit(solution)/shard_map/finish/pallas_call | solution.py:568

commit v4 on v3

--- a/solution.py
+++ b/solution.py
@@ -32,10 +32,10 @@
 
 
 def kernel(
-    u_in, b_in, span_in, coef, xb_in, yb_in, zb_in, vx_in, vy_in, vz_in, xv_in, yv_in, zv_in,
+    u_in, b_in, span_in, coef_in, xb_in, yb_in, zb_in, vx_in, vy_in, vz_in, xv_in, yv_in, zv_in,
     u_out, r_out,
-    u, b, span, vx, vy, vz, xb, yb, zb, xv, yv, zv, c, r, zs, cs, hc, rl, hr, w, acc,
-    s, ra, sb, rb, rc, se, rd, m, mb, rb2, sa2, rm, sn, ra2,
+    u, b, span, vx, vy, vz, xb, yb, zb, xv, yv, zv, coef, c, r, zs, cs, hc, rl, hr, w, acc,
+    s, ra, sb, rb, rc, se, rd, m, mz, mg, rz, rg, sg, ry, sz, rx, ra2,
     bm_h, bm_l, vxt_h, vxt_l, vy_h, vy_l, vyt_h, vyt_l, vz_h, vz_l, den,
     kx_h, kx_l, mx_h, mx_l, load_sem, send_sem, recv_sem,
 ):
@@ -66,11 +66,11 @@
         pltpu.make_async_copy(src, dst, load_sem.at[i])
         for i, (src, dst) in enumerate(
             ((u_in, u), (span_in, span), (vx_in, vx), (vy_in, vy), (vz_in, vz), (b_in, b),
-             (xb_in, xb), (yb_in, yb), (zb_in, zb), (xv_in, xv), (yv_in, yv), (zv_in, zv))
+             (xb_in, xb), (yb_in, yb), (zb_in, zb), (xv_in, xv), (yv_in, yv), (zv_in, zv), (coef_in, coef))
         )
     ]
-    loads[0].start()
-    loads[1].start()
+    for i in (0, 1, 12):
+        loads[i].start()
     barrier = pltpu.get_barrier_semaphore()
 
     def greet(k, carry):
@@ -99,7 +99,7 @@
         for k in range(1, 4):
             pl.semaphore_signal(barrier, inc=1, device_id=device(above + 2 * k, pz))
 
-    for load in loads[2:]:
+    for load in loads[2:12]:
         load.start()
     cs[...] = jnp.zeros_like(cs)
     for it in range(ITERS):
@@ -107,13 +107,15 @@
 
     loads[0].wait()
     loads[1].wait()
+    loads[12].wait()
+    table = [coef[:, e : e + 1] for e in range(8)]
 
     def weigh(i, carry):
         rows = pl.ds(pl.multiple_of(i * 8, 8), 8)
         at = span[rows, :]
-        v = jnp.full((8, 512), coef[0], F32)
+        v = jnp.broadcast_to(table[0], (8, 512))
         for e in range(1, 8):
-            v = jnp.where(at == e, coef[e], v)
+            v = jnp.where(at == e, table[e], v)
         c[rows, :] = v
         w[0, rows, :] = v * u[rows, :]
         return carry
@@ -320,7 +322,7 @@
 
         @pl.when(it == ITERS - 1)
         def _():
-            pltpu.make_async_copy(r, r_out, load_sem.at[12]).start()
+            pltpu.make_async_copy(r, r_out, load_sem.at[13]).start()
 
         turned = [r[((8 - i) % 8) * 16 : ((8 - i) % 8) * 16 + 16, :] for i in range(8)]
         wide = split(jnp.concatenate(turned, axis=0))
@@ -345,9 +347,9 @@
         modes(0)
         modes(1)
 
-        def send_some(src, dst, stage, where, count, own, source=lambda i: i):
+        def send_some(src, dst, stage, where, own, source=lambda i: i):
             def one(k, carry):
-                i = (mine + k) % count if count == 16 else (g + k) % 32
+                i = (mine + k) % 16
 
                 @pl.when(i != own)
                 def _():
@@ -355,7 +357,7 @@
 
                 return carry
 
-            lax.fori_loop(0, count, one, 0)
+            lax.fori_loop(0, 16, one, 0)
 
         def first_core(i):
             return device(zh * 8 + (i // 4) * 2, (i % 4) * 4 + zl)
@@ -364,7 +366,7 @@
             return device(zh * 8 + (i // 4) * 2 + 1, (i % 4) * 4 + zl)
 
         none = 99
-        send_some(s, ra.at[it, block(g)], 1, first_core, 16, jnp.where(first, mine, none))
+        send_some(s, ra.at[it, block(g)], 1, first_core, jnp.where(first, mine, none))
 
         @pl.when(first)
         def _():
@@ -380,7 +382,7 @@
         wait_rows(rc.at[it, 0 : 15 * 16], 2)
         for k in range(16):
             se[it, k * 16 : k * 16 + 16, :] = rc[it, pl.ds(k, 16, stride=16), :]
-        send_some(se, rd.at[it, block(g)], 4, second_core, 16, jnp.where(second, mine, none))
+        send_some(se, rd.at[it, block(g)], 4, second_core, jnp.where(second, mine, none))
 
         @pl.when(first)
         def _():
@@ -409,63 +411,62 @@
         m[...] = dot3(split(m[...]), vzs, ((1,), (1,)))
 
         for t in range(4):
-            rows = slice(t * 8, t * 8 + 8)
             for h in range(4):
                 one, two = ((h * 8 + yy) * 8 for yy in PLACES[t])
                 for p in range(2):
                     low, high = m[one : one + 8, quarter[p]], m[two : two + 8, quarter[p]]
-                    a = jnp.where(lane < 64, low, pltpu.roll(high, 64, 1))
-                    e = jnp.where(lane < 64, pltpu.roll(low, 64, 1), high)
-                    mb[it, h * 4 + 2 * p, rows, :] = swap_blocks(a, lane)
-                    mb[it, h * 4 + 2 * p + 1, rows, :] = swap_blocks(e, lane)
+                    pair = (
+                        jnp.where(lane < 64, low, pltpu.roll(high, 64, 1)),
+                        jnp.where(lane < 64, pltpu.roll(low, 64, 1), high),
+                    )
+                    for e, v in enumerate(pair):
+                        v = pltpu.roll(swap_blocks(v, lane), 3, 0)
+                        k = h * 4 + 2 * p + e
+                        mz[it, k * 16 + t * 4 : k * 16 + t * 4 + 4, :] = v[0:4]
+                        mg[it, pl.ds(t * 64 + k, 4, stride=16), :] = v[4:8]
+        for k in RING:
+            q2 = (q + k) % 16
+            push(it, mz.at[it, block(q2)], rz.at[it, block(q)], 8, ring(q2))
+        rz[it, block(q), :] = mz[it, block(q), :]
 
         def turn(i):
-            return (i // 8) * 8 + (8 - i % 8) % 8
-
-        def by_group(src, dst):
+            return (i // 4) * 4 + 3 - i % 4
+
+        slot = core * 16 + mine
+        send_some(mg, rg.at[it, block(slot)], 10, second_core, jnp.where(second, mine, none), turn)
+
+        @pl.when(second)
+        def _():
+            rg[it, block(slot), :] = mg[it, block(turn(mine)), :]
+            wait_rows(rg.at[it, 0 : 31 * 16], 10)
             for k in range(16):
-                for h in range(4):
-                    dst[it, pl.ds(h * 128 + k, 8, stride=16), :] = src[it, k, h * 8 : h * 8 + 8, :]
-
-        @pl.when(first)
-        def _():
+                sg[it, k] = rg[it, pl.ds(k, 32, stride=16), :]
             for k in RING:
                 q2 = (q + k) % 16
-                push(it, mb.at[it, q2], rb2.at[it, q], 8, ring(q2))
-            rb2[it, q] = mb[it, q]
+                push(it, sg.at[it, q2], ry.at[it, q], 11, ring(q2))
+            ry[it, q] = sg[it, q]
+
+        wait_rows(rz.at[it, 0 : 15 * 16], 8)
+        for k in range(16):
+            sz[it, k * 16 : k * 16 + 16, :] = rz[it, pl.ds(k, 16, stride=16), :]
+        send_some(sz, rx.at[it, block(slot)], 9, first_core, jnp.where(first, mine, none), turn)
+
+        @pl.when(first)
+        def _():
+            rx[it, block(slot), :] = sz[it, block(turn(mine)), :]
+            wait_rows(rx.at[it, 0 : 31 * 16], 9)
+            ra2[0:256, :] = rx[it, 0:256, :]
+            for k in range(16):
+                ra2[256 + k * 16 : 272 + k * 16, :] = rx[it, pl.ds(256 + k, 16, stride=16), :]
 
         @pl.when(second)
         def _():
-            by_group(mb, sa2)
-            send_some(sa2, rm.at[it, block(mine)], 10, group, 32, g, turn)
-            rm[it, block(mine), :] = sa2[it, block(turn(g)), :]
-            wait_rows(rm.at[it, 0 : 15 * 16], 10)
-
-        @pl.when(first)
-        def _():
-            wait_rows(rm.at[it, 0 : 16 * 16], 10)
-
-        for k in range(16):
-            sn[it, k * 16 : k * 16 + 16, :] = rm[it, pl.ds(k, 16, stride=16), :]
-        for k in RING:
-            q2 = (q + k) % 16
-            push(it, sn.at[it, block(q2)], ra2.at[it, block(16 + q)], 11, ring(q2))
-        ra2[it, block(16 + q), :] = sn[it, block(q), :]
-
-        @pl.when(first)
-        def _():
-            wait_rows(rb2.at[it, 0:15], 8)
-            by_group(rb2, sa2)
-            send_some(sa2, ra2.at[it, block(mine)], 9, group, 32, g, turn)
-            ra2[it, block(mine), :] = sa2[it, block(turn(g)), :]
-            wait_rows(ra2.at[it, 0 : 15 * 16], 9)
-
-        @pl.when(second)
-        def _():
-            wait_rows(ra2.at[it, 0 : 16 * 16], 9)
-
-        wait_rows(ra2.at[it, 0 : 15 * 16], 11)
-        wide = split(jnp.transpose(ra2[it]))
+            wait_rows(ry.at[it, 0:15], 11)
+            for k in range(16):
+                ra2[256 + k * 16 : 272 + k * 16, :] = ry[it, k, 16:32, :]
+                ra2[pl.ds(k, 16, stride=16), :] = ry[it, k, 0:16, :]
+
+        wide = split(jnp.transpose(ra2[...]))
         u[...] += dot3(wide, (vxt_h[...], vxt_l[...]))
 
         @pl.when(it + 1 < ITERS)
@@ -477,7 +478,7 @@
         return carry
 
     lax.fori_loop(0, ITERS, step, 0)
-    last = pltpu.make_async_copy(u, u_out, load_sem.at[13])
+    last = pltpu.make_async_copy(u, u_out, load_sem.at[14])
     last.start()
     for it in range(ITERS):
         @pl.when(jnp.logical_not(top | bottom))
@@ -503,24 +504,26 @@
 
         sent(6, hc.at[it])
         sent(2, ra.at[it, 0 : 15 * 16])
-        sent(11, ra.at[it, 0 : 15 * 16])
+        sent(8, ra.at[it, 0 : 15 * 16])
 
         @pl.when(first)
         def _(it=it, sent=sent):
             sent(1, ra.at[it, 0 : 15 * 16])
             sent(3, sb.at[it, 0:15])
             sent(4, ra.at[it, 0 : 16 * 16])
-            sent(8, sb.at[it, 0:15])
-            sent(9, ra.at[it, 0 : 31 * 16])
+            sent(10, ra.at[it, 0 : 16 * 16])
+            sent(9, ra.at[it, 0 : 15 * 16])
 
         @pl.when(second)
         def _(it=it, sent=sent):
             sent(1, ra.at[it, 0 : 16 * 16])
             sent(4, ra.at[it, 0 : 15 * 16])
-            sent(10, ra.at[it, 0 : 31 * 16])
+            sent(10, ra.at[it, 0 : 15 * 16])
+            sent(11, sb.at[it, 0:15])
+            sent(9, ra.at[it, 0 : 16 * 16])
 
     last.wait()
-    pltpu.make_async_copy(r, r_out, load_sem.at[12]).wait()
+    pltpu.make_async_copy(r, r_out, load_sem.at[13]).wait()
 
 
 def finish(u_in, r_in, u_out, r_out):
@@ -533,34 +536,33 @@
     flat = (128, 512)
     hbm = pl.BlockSpec(memory_space=pl.ANY)
     vmem = pl.BlockSpec(memory_space=pltpu.VMEM)
-    smem = pl.BlockSpec(memory_space=pltpu.SMEM)
     V = pltpu.VMEM
     big = V((ITERS, 512, 128), F32)
     half = V((ITERS, 256, 128), F32)
     ring = V((ITERS, 16, 32, 128), F32)
     scratch = [
         V(flat, F32), V(flat, F32), V(flat, jnp.int32), V((512, 512), F32), V((256, 256), F32), V((256, 256), F32),
-        V((7, 2, 512), F32), V((7, 2, 8), F32), V((7, 2, 16), F32), V((1, 512), F32), V((1, 256), F32), V((1, 256), F32),
+        V((7, 2, 512), F32), V((7, 2, 8), F32), V((7, 2, 16), F32), V((1, 512), F32), V((1, 256), F32), V((1, 256), F32), V((1, 8), F32),
         V(flat, F32), V(flat, F32), V((ITERS, 2, 24, 512), F32), V((ITERS, 4, 40, 128), F32),
         V((ITERS, 4, 40, 128), F32), V((ITERS, 48, 128), F32),
         V((ITERS, 256, 512), F32), V((ITERS, 128, 512), F32), V((256, 512), F32),
-        big, big, ring, ring, half, half, big, V((256, 256), F32), ring, ring, big, half, half, big,
+        big, big, ring, ring, half, half, big, V((256, 256), F32), half, half, half, big, ring, ring, half, big, V((512, 128), F32),
         V((256, 384), BF16), V((256, 384), BF16), V((512, 512), BF16), V((512, 512), BF16),
         V((256, 256), BF16), V((256, 256), BF16), V((256, 256), BF16), V((256, 256), BF16),
         V((256, 256), BF16), V((256, 256), BF16), V((256, 256), F32),
         V((512, 512), BF16), V((512, 512), BF16), V((512, 512), BF16), V((512, 512), BF16),
-        pltpu.SemaphoreType.DMA((14,)), pltpu.SemaphoreType.DMA((ITERS, 12)), pltpu.SemaphoreType.DMA((ITERS, 12)),
+        pltpu.SemaphoreType.DMA((15,)), pltpu.SemaphoreType.DMA((ITERS, 12)), pltpu.SemaphoreType.DMA((ITERS, 12)),
     ]
     updated, residual = pl.pallas_call(
         kernel,
         out_shape=(jax.ShapeDtypeStruct(flat, F32), jax.ShapeDtypeStruct(flat, F32)),
-        in_specs=[hbm, hbm, hbm, smem] + [hbm] * 9,
+        in_specs=[hbm] * 13,
         out_specs=(hbm, hbm),
         scratch_shapes=scratch,
         compiler_params=pltpu.CompilerParams(collective_id=0, has_side_effects=True),
         name="richardson",
     )(
-        solution.reshape(flat), right_side.reshape(flat), span_index.reshape(flat), coef_table,
+        solution.reshape(flat), right_side.reshape(flat), span_index.reshape(flat), coef_table.reshape(1, 8),
         jnp.swapaxes(xaxis_bands, 0, 1), jnp.swapaxes(yaxis_bands, 0, 1), jnp.swapaxes(zaxis_bands, 0, 1),
         xaxis_vectors, yaxis_vectors, zaxis_vectors,
         xaxis_values.reshape(1, 512), yaxis_values.reshape(1, 256), zaxis_values.reshape(1, 256),

time: 115 us -> 107 us (0.930)
  Pallas kernels: 114 us -> 106 us
    pallas_call x1, Pallas kernels: 113 us -> 104 us  [shards(): pl.pallas_call(kernel, out_shape=(jax.ShapeDtypeStruct(flat, F32), jax.Sh...]
where the time goes in v4:
time: 107 us
  Pallas kernels  106 us (99%)
    pallas_call x1, Pallas kernels, shards(): pl.pallas_call(kernel, out_shape=(jax.ShapeDtypeStruct(flat, F32), jax.Sh...  104 us

profile of v4, /device:TPU:1, one launch (start us, length us, event | category | flops | bytes accessed | tf_op | source)
XLA Modules:
  0.0 106.6 jit_solution(920456615915366774)
XLA Ops:
  0.6 104.2 %richardson.1 = (f32[128,512]{1,0:T(8,128)}, f32[128,512]{1,0:T(8,128)}) custom-call(f32[128,512]{1,0:T(8,128)} %bitcast.12, f32[128,512]{1,0:T(8,128)} %bitcast.13, s32[128,512]{1,0:T(8,128)} %bitcast.14, f32[1,8]{1,0:T(1,128)} %bitcast.21, f32[7,2,512]{2,1,0:T(2,128)} %bitcast.15, f32[7,2,8]{2,1,0:T(2,128)} %bitcast.16, f32[7,2,16]{2,1,0:T(2,128)} %bitcast.17, ...), custom_call_target="tpu_custom_call" | custom-call | tf_op jit(solution)/shard_map/richardson/pallas_call | solution.py:556
  104.8 1.8 %finish.1 = (f32[128,512]{1,0:T(8,128)}, f32[128,512]{1,0:T(8,128)}) custom-call(f32[128,512]{1,0:T(8,128)} %get-tuple-element.6.u_in, f32[128,512]{1,0:T(8,128)} %get-tuple-element.7.r_in), custom_call_target="tpu_custom_call" | custom-call | tf_op jit(solution)/shard_map/finish/pallas_call | solution.py:570

commit v5 on v4

--- a/solution.py
+++ b/solution.py
@@ -69,21 +69,11 @@
              (xb_in, xb), (yb_in, yb), (zb_in, zb), (xv_in, xv), (yv_in, yv), (zv_in, zv), (coef_in, coef))
         )
     ]
+    barrier = pltpu.get_barrier_semaphore()
+    for k in RING:
+        pl.semaphore_signal(barrier, inc=1, device_id=ring((q + k) % 16))
     for i in (0, 1, 12):
         loads[i].start()
-    barrier = pltpu.get_barrier_semaphore()
-
-    def greet(k, carry):
-        pl.semaphore_signal(barrier, inc=1, device_id=group((g + k) % 32))
-        return carry
-
-    lax.fori_loop(1, 32, greet, 0)
-
-    def greet_ring(k, carry):
-        pl.semaphore_signal(barrier, inc=1, device_id=ring((q + k) % 16))
-        return carry
-
-    lax.fori_loop(1, 16, greet_ring, 0)
     sides = [(dy, dz) for dy in (-1, 0, 1) for dz in (-1, 0, 1) if dy or dz]
     for dy, dz in sides:
         pl.semaphore_signal(barrier, inc=1, device_id=near(dy, dz))
@@ -91,14 +81,17 @@
 
     @pl.when(bottom)
     def _():
-        for k in range(3):
-            pl.semaphore_signal(barrier, inc=1, device_id=device(below + 2 * k + 1, pz))
+        pl.semaphore_signal(barrier, inc=1, device_id=device(below + 1, pz))
 
     @pl.when(top)
     def _():
-        for k in range(1, 4):
-            pl.semaphore_signal(barrier, inc=1, device_id=device(above + 2 * k, pz))
-
+        pl.semaphore_signal(barrier, inc=1, device_id=device(above + 6, pz))
+
+    def greet(k, carry):
+        pl.semaphore_signal(barrier, inc=1, device_id=group((g + k) % 32))
+        return carry
+
+    lax.fori_loop(1, 32, greet, 0)
     for load in loads[2:12]:
         load.start()
     cs[...] = jnp.zeros_like(cs)
@@ -121,7 +114,7 @@
         return carry
 
     lax.fori_loop(0, 16, weigh, 0)
-    pl.semaphore_wait(barrier, 31 + 15 + 8 + jnp.where(top | bottom, 0, 1))
+    pl.semaphore_wait(barrier, 31 + 15 + 8 + jnp.where((yc == 1) | (yc == 6), 1, 0))
 
     sub = lax.broadcasted_iota(jnp.int32, (8, 128), 0)
     lane = lax.broadcasted_iota(jnp.int32, (8, 128), 1)
@@ -254,46 +247,55 @@
                         at = t * 9 + i * 3
                         cs[it, cy * 2 + cz, at : at + 3, :] = three[:, t * 128 : t * 128 + 128]
         own = w.at[it]
+        left, right = slice(0, 256), slice(256, 512)
 
         @pl.when(top)
         def _():
-            for k in range(3):
-                push(it, own.at[80:128, quarter[k]], rl.at[it], 5, device(zh * 8 + 2 * k + 1, pz))
-            push(it, own.at[80:128, quarter[3]], hr.at[it, 0:48, quarter[3]], 0, near(1, 0), 5)
+            push(it, own.at[80:128, left], rl.at[it], 5, device(zh * 8 + 1, pz))
 
         @pl.when(bottom)
         def _():
-            for k in range(1, 4):
-                push(it, own.at[0:48, quarter[k]], rl.at[it], 5, device(zh * 8 + 2 * k, pz))
-            push(it, own.at[0:48, quarter[0]], hr.at[it, 48:96, quarter[0]], 0, near(-1, 0), 5)
+            push(it, own.at[0:48, right], rl.at[it], 5, device(zh * 8 + 6, pz))
+
+        push(it, zs.at[it, 1], hr.at[it, 96:120], 0, near(0, 1))
+        push(it, zs.at[it, 0], hr.at[it, 120:144], 0, near(0, -1))
+
+        @pl.when(top)
+        def _():
+            push(it, own.at[80:128, right], hr.at[it, 0:48, right], 0, near(1, 0), 5)
+
+        @pl.when(bottom)
+        def _():
+            push(it, own.at[0:48, left], hr.at[it, 48:96, left], 0, near(-1, 0), 5)
+
+        @pl.when(jnp.logical_not(top))
+        def _():
+            push(it, own.at[80:128], hr.at[it, 0:48], 0, near(1, 0))
+
+        @pl.when(jnp.logical_not(bottom))
+        def _():
+            push(it, own.at[0:48], hr.at[it, 48:96], 0, near(-1, 0))
 
         push(it, cs.at[it, 3], hc.at[it, 0], 6, near(1, 1))
         push(it, cs.at[it, 2], hc.at[it, 1], 6, near(1, -1))
         push(it, cs.at[it, 1], hc.at[it, 2], 6, near(-1, 1))
         push(it, cs.at[it, 0], hc.at[it, 3], 6, near(-1, -1))
 
-        @pl.when(jnp.logical_not(top))
-        def _():
-            push(it, own.at[80:128], hr.at[it, 0:48], 0, near(1, 0))
-
-        @pl.when(jnp.logical_not(bottom))
-        def _():
-            push(it, own.at[0:48], hr.at[it, 48:96], 0, near(-1, 0))
-
-        push(it, zs.at[it, 1], hr.at[it, 96:120], 0, near(0, 1))
-        push(it, zs.at[it, 0], hr.at[it, 120:144], 0, near(0, -1))
-
     def relay(it):
-        @pl.when(jnp.logical_not(top | bottom))
-        def _():
+        def passed():
             pltpu.make_async_remote_copy(
                 rl.at[it], rl.at[it], send_sem.at[it, 5], recv_sem.at[it, 5], device_id=near(1, 0)
             ).wait_recv()
-            odd = yc % 2 == 1
-            start = pl.multiple_of(jnp.where(odd, 0, 48), 8)
-            cols = pl.ds(pl.multiple_of((yc // 2) * 128, 128), 128)
-            push(it, rl.at[it], hr.at[it, pl.ds(start, 48), cols], 0,
-                 device(jnp.where(odd, above, below + 7), pz), 7)
+
+        @pl.when(yc == 1)
+        def _():
+            passed()
+            push(it, rl.at[it], hr.at[it, 0:48, 0:256], 0, device(above, pz), 7)
+
+        @pl.when(yc == 6)
+        def _():
+            passed()
+            push(it, rl.at[it], hr.at[it, 48:96, 256:512], 0, device(below + 7, pz), 7)
 
     rims(0)
     relay(0)
@@ -322,7 +324,7 @@
 
         @pl.when(it == ITERS - 1)
         def _():
-            pltpu.make_async_copy(r, r_out, load_sem.at[13]).start()
+            r_out[...] = r[...]
 
         turned = [r[((8 - i) % 8) * 16 : ((8 - i) % 8) * 16 + 16, :] for i in range(8)]
         wide = split(jnp.concatenate(turned, axis=0))
@@ -338,35 +340,34 @@
                 part, part, send_sem.at[it, 0], recv_sem.at[it, stage], device_id=near(1, 0)
             ).wait_recv()
 
+        def send_some(src, dst, stage, where, own, source=lambda i: i):
+            def one(k, carry):
+                i = (mine + k) % 16
+
+                @pl.when(i != own)
+                def _():
+                    push(it, src.at[it, block(source(i))], dst, stage, where(i))
+
+                return carry
+
+            lax.fori_loop(0, 16, one, 0)
+
+        def first_core(i):
+            return device(zh * 8 + (i // 4) * 2, (i % 4) * 4 + zl)
+
+        def second_core(i):
+            return device(zh * 8 + (i // 4) * 2 + 1, (i % 4) * 4 + zl)
+
+        none = 99
+        modes(0)
+        modes(1)
+        send_some(s, ra.at[it, block(g)], 1, first_core, jnp.where(first, mine, none))
         modes(2)
         modes(3)
         for k in RING:
             q2 = (q + k) % 16
             push(it, s.at[it, block(16 + q2)], rc.at[it, block(q)], 2, ring(q2))
         rc[it, block(q), :] = s[it, block(16 + q), :]
-        modes(0)
-        modes(1)
-
-        def send_some(src, dst, stage, where, own, source=lambda i: i):
-            def one(k, carry):
-                i = (mine + k) % 16
-
-                @pl.when(i != own)
-                def _():
-                    push(it, src.at[it, block(source(i))], dst, stage, where(i))
-
-                return carry
-
-            lax.fori_loop(0, 16, one, 0)
-
-        def first_core(i):
-            return device(zh * 8 + (i // 4) * 2, (i % 4) * 4 + zl)
-
-        def second_core(i):
-            return device(zh * 8 + (i // 4) * 2 + 1, (i % 4) * 4 + zl)
-
-        none = 99
-        send_some(s, ra.at[it, block(g)], 1, first_core, jnp.where(first, mine, none))
 
         @pl.when(first)
         def _():
@@ -424,16 +425,15 @@
                         k = h * 4 + 2 * p + e
                         mz[it, k * 16 + t * 4 : k * 16 + t * 4 + 4, :] = v[0:4]
                         mg[it, pl.ds(t * 64 + k, 4, stride=16), :] = v[4:8]
+        def turn(i):
+            return (i // 4) * 4 + 3 - i % 4
+
+        slot = core * 16 + mine
+        send_some(mg, rg.at[it, block(slot)], 10, second_core, jnp.where(second, mine, none), turn)
         for k in RING:
             q2 = (q + k) % 16
             push(it, mz.at[it, block(q2)], rz.at[it, block(q)], 8, ring(q2))
         rz[it, block(q), :] = mz[it, block(q), :]
-
-        def turn(i):
-            return (i // 4) * 4 + 3 - i % 4
-
-        slot = core * 16 + mine
-        send_some(mg, rg.at[it, block(slot)], 10, second_core, jnp.where(second, mine, none), turn)
 
         @pl.when(second)
         def _():
@@ -469,6 +469,10 @@
         wide = split(jnp.transpose(ra2[...]))
         u[...] += dot3(wide, (vxt_h[...], vxt_l[...]))
 
+        @pl.when(it == ITERS - 1)
+        def _():
+            u_out[...] = u[...]
+
         @pl.when(it + 1 < ITERS)
         def _():
             w[it + 1] = c[...] * u[...]
@@ -478,14 +482,15 @@
         return carry
 
     lax.fori_loop(0, ITERS, step, 0)
-    last = pltpu.make_async_copy(u, u_out, load_sem.at[14])
-    last.start()
     for it in range(ITERS):
         @pl.when(jnp.logical_not(top | bottom))
         def _(it=it):
             pltpu.make_async_remote_copy(
                 hr.at[it, 0:144], hr.at[it, 0:144], send_sem.at[it, 0], recv_sem.at[it, 0], device_id=near(1, 0)
             ).wait_send()
+
+        @pl.when((yc == 1) | (yc == 6))
+        def _(it=it):
             pltpu.make_async_remote_copy(
                 rl.at[it], rl.at[it], send_sem.at[it, 7], recv_sem.at[it, 0], device_id=near(1, 0)
             ).wait_send()
@@ -522,9 +527,6 @@
             sent(11, sb.at[it, 0:15])
             sent(9, ra.at[it, 0 : 16 * 16])
 
-    last.wait()
-    pltpu.make_async_copy(r, r_out, load_sem.at[13]).wait()
-
 
 def finish(u_in, r_in, u_out, r_out):
     u_out[...] = u_in[...]
@@ -534,7 +536,7 @@
 def shards(solution, right_side, span_index, coef_table, xaxis_bands, yaxis_bands, zaxis_bands,
            xaxis_vectors, yaxis_vectors, zaxis_vectors, xaxis_values, yaxis_values, zaxis_values):
     flat = (128, 512)
-    hbm = pl.BlockSpec(memory_space=pl.ANY)
+    hbm = pl.BlockSpec(memory_space=pltpu.HBM)
     vmem = pl.BlockSpec(memory_space=pltpu.VMEM)
     V = pltpu.VMEM
     big = V((ITERS, 512, 128), F32)
@@ -544,34 +546,35 @@
         V(flat, F32), V(flat, F32), V(flat, jnp.int32), V((512, 512), F32), V((256, 256), F32), V((256, 256), F32),
         V((7, 2, 512), F32), V((7, 2, 8), F32), V((7, 2, 16), F32), V((1, 512), F32), V((1, 256), F32), V((1, 256), F32), V((1, 8), F32),
         V(flat, F32), V(flat, F32), V((ITERS, 2, 24, 512), F32), V((ITERS, 4, 40, 128), F32),
-        V((ITERS, 4, 40, 128), F32), V((ITERS, 48, 128), F32),
+        V((ITERS, 4, 40, 128), F32), V((ITERS, 48, 256), F32),
         V((ITERS, 256, 512), F32), V((ITERS, 128, 512), F32), V((256, 512), F32),
         big, big, ring, ring, half, half, big, V((256, 256), F32), half, half, half, big, ring, ring, half, big, V((512, 128), F32),
         V((256, 384), BF16), V((256, 384), BF16), V((512, 512), BF16), V((512, 512), BF16),
         V((256, 256), BF16), V((256, 256), BF16), V((256, 256), BF16), V((256, 256), BF16),
         V((256, 256), BF16), V((256, 256), BF16), V((256, 256), F32),
         V((512, 512), BF16), V((512, 512), BF16), V((512, 512), BF16), V((512, 512), BF16),
-        pltpu.SemaphoreType.DMA((15,)), pltpu.SemaphoreType.DMA((ITERS, 12)), pltpu.SemaphoreType.DMA((ITERS, 12)),
+        pltpu.SemaphoreType.DMA((13,)), pltpu.SemaphoreType.DMA((ITERS, 12)), pltpu.SemaphoreType.DMA((ITERS, 12)),
     ]
     updated, residual = pl.pallas_call(
         kernel,
         out_shape=(jax.ShapeDtypeStruct(flat, F32), jax.ShapeDtypeStruct(flat, F32)),
         in_specs=[hbm] * 13,
-        out_specs=(hbm, hbm),
+        out_specs=(vmem, vmem),
         scratch_shapes=scratch,
-        compiler_params=pltpu.CompilerParams(collective_id=0, has_side_effects=True),
+        compiler_params=pltpu.CompilerParams(collective_id=0, has_side_effects=True, vmem_limit_bytes=24 * 1024 * 1024),
         name="richardson",
-    )(
+    )(*(pltpu.with_memory_space_constraint(a, pltpu.HBM) for a in (
         solution.reshape(flat), right_side.reshape(flat), span_index.reshape(flat), coef_table.reshape(1, 8),
         jnp.swapaxes(xaxis_bands, 0, 1), jnp.swapaxes(yaxis_bands, 0, 1), jnp.swapaxes(zaxis_bands, 0, 1),
         xaxis_vectors, yaxis_vectors, zaxis_vectors,
         xaxis_values.reshape(1, 512), yaxis_values.reshape(1, 256), zaxis_values.reshape(1, 256),
-    )
+    )))
     updated, residual = pl.pallas_call(
         finish,
         out_shape=(jax.ShapeDtypeStruct(flat, F32), jax.ShapeDtypeStruct(flat, F32)),
         in_specs=[vmem, vmem],
         out_specs=(vmem, vmem),
+        compiler_params=pltpu.CompilerParams(vmem_limit_bytes=8 * 1024 * 1024),
         name="finish",
     )(updated, residual)
     return updated.reshape(solution.shape), residual.reshape(solution.shape)

time: 107 us -> 108 us (level)
    pallas_call x1, Pallas kernels: 104 us -> 106 us  [shards(): pl.pallas_call(kernel, out_shape=(jax.ShapeDtypeStruct(flat, F32), jax.Sh...]
where the time goes in v5:
time: 108 us
  Pallas kernels  107 us (99%)
    pallas_call x1, Pallas kernels, shards(): pl.pallas_call(kernel, out_shape=(jax.ShapeDtypeStruct(flat, F32), jax.Sh...  106 us

profile of v5, /device:TPU:1, one launch (start us, length us, event | category | flops | bytes accessed | tf_op | source)
XLA Modules:
  0.0 107.8 jit_solution(1998618688647778112)
XLA Ops:
  0.6 106.3 %richardson.1 = (f32[128,512]{1,0:T(8,128)S(1)}, f32[128,512]{1,0:T(8,128)S(1)}) custom-call(f32[128,512]{1,0:T(8,128)} %bitcast.12, f32[128,512]{1,0:T(8,128)} %bitcast.13, s32[128,512]{1,0:T(8,128)} %bitcast.14, f32[1,8]{1,0:T(1,128)} %bitcast.21, f32[7,2,512]{2,1,0:T(2,128)} %bitcast.15, f32[7,2,8]{2,1,0:T(2,128)} %bitcast.16, f32[7,2,16]{2,1,0:T(2,128)} %bitcast.17, ...), custom_call_target="tpu_custom_call" | custom-call | tf_op jit(solution)/shard_map/richardson/pallas_call | solution.py:558
  107.0 0.8 finish.1

commit v6 on v4

--- a/solution.py
+++ b/solution.py
@@ -9,6 +9,7 @@
 F32 = jnp.float32
 BF16 = jnp.bfloat16
 PLACES = ((0, 1), (2, 3), (4, 5), (6, 7))
+FAR = ((2, 2), (2, 1), (1, 2), (2, 3), (3, 2), (0, 2), (2, 0), (1, 1), (1, 3), (3, 1), (3, 3), (0, 1), (1, 0), (0, 3), (3, 0))
 RING = (8, 7, 9, 6, 10, 5, 11, 4, 12, 3, 13, 2, 14, 1, 15)
 
 
@@ -69,21 +70,11 @@
              (xb_in, xb), (yb_in, yb), (zb_in, zb), (xv_in, xv), (yv_in, yv), (zv_in, zv), (coef_in, coef))
         )
     ]
+    barrier = pltpu.get_barrier_semaphore()
+    for k in RING:
+        pl.semaphore_signal(barrier, inc=1, device_id=ring((q + k) % 16))
     for i in (0, 1, 12):
         loads[i].start()
-    barrier = pltpu.get_barrier_semaphore()
-
-    def greet(k, carry):
-        pl.semaphore_signal(barrier, inc=1, device_id=group((g + k) % 32))
-        return carry
-
-    lax.fori_loop(1, 32, greet, 0)
-
-    def greet_ring(k, carry):
-        pl.semaphore_signal(barrier, inc=1, device_id=ring((q + k) % 16))
-        return carry
-
-    lax.fori_loop(1, 16, greet_ring, 0)
     sides = [(dy, dz) for dy in (-1, 0, 1) for dz in (-1, 0, 1) if dy or dz]
     for dy, dz in sides:
         pl.semaphore_signal(barrier, inc=1, device_id=near(dy, dz))
@@ -99,6 +90,11 @@
         for k in range(1, 4):
             pl.semaphore_signal(barrier, inc=1, device_id=device(above + 2 * k, pz))
 
+    def greet(k, carry):
+        pl.semaphore_signal(barrier, inc=1, device_id=group((g + k) % 32))
+        return carry
+
+    lax.fori_loop(1, 32, greet, 0)
     for load in loads[2:12]:
         load.start()
     cs[...] = jnp.zeros_like(cs)
@@ -322,7 +318,7 @@
 
         @pl.when(it == ITERS - 1)
         def _():
-            pltpu.make_async_copy(r, r_out, load_sem.at[13]).start()
+            r_out[...] = r[...]
 
         turned = [r[((8 - i) % 8) * 16 : ((8 - i) % 8) * 16 + 16, :] for i in range(8)]
         wide = split(jnp.concatenate(turned, axis=0))
@@ -348,16 +344,13 @@
         modes(1)
 
         def send_some(src, dst, stage, where, own, source=lambda i: i):
-            def one(k, carry):
-                i = (mine + k) % 16
-
-                @pl.when(i != own)
-                def _():
-                    push(it, src.at[it, block(source(i))], dst, stage, where(i))
-
-                return carry
-
-            lax.fori_loop(0, 16, one, 0)
+            for dy, dx in FAR:
+                i = ((mine // 4 + dy) % 4) * 4 + (mine % 4 + dx) % 4
+                push(it, src.at[it, block(source(i))], dst, stage, where(i))
+
+            @pl.when(mine != own)
+            def _():
+                push(it, src.at[it, block(source(mine))], dst, stage, where(mine))
 
         def first_core(i):
             return device(zh * 8 + (i // 4) * 2, (i % 4) * 4 + zl)
@@ -469,6 +462,10 @@
         wide = split(jnp.transpose(ra2[...]))
         u[...] += dot3(wide, (vxt_h[...], vxt_l[...]))
 
+        @pl.when(it == ITERS - 1)
+        def _():
+            u_out[...] = u[...]
+
         @pl.when(it + 1 < ITERS)
         def _():
             w[it + 1] = c[...] * u[...]
@@ -478,8 +475,6 @@
         return carry
 
     lax.fori_loop(0, ITERS, step, 0)
-    last = pltpu.make_async_copy(u, u_out, load_sem.at[14])
-    last.start()
     for it in range(ITERS):
         @pl.when(jnp.logical_not(top | bottom))
         def _(it=it):
@@ -521,9 +516,6 @@
             sent(10, ra.at[it, 0 : 15 * 16])
             sent(11, sb.at[it, 0:15])
             sent(9, ra.at[it, 0 : 16 * 16])
-
-    last.wait()
-    pltpu.make_async_copy(r, r_out, load_sem.at[13]).wait()
 
 
 def finish(u_in, r_in, u_out, r_out):
@@ -551,27 +543,28 @@
         V((256, 256), BF16), V((256, 256), BF16), V((256, 256), BF16), V((256, 256), BF16),
         V((256, 256), BF16), V((256, 256), BF16), V((256, 256), F32),
         V((512, 512), BF16), V((512, 512), BF16), V((512, 512), BF16), V((512, 512), BF16),
-        pltpu.SemaphoreType.DMA((15,)), pltpu.SemaphoreType.DMA((ITERS, 12)), pltpu.SemaphoreType.DMA((ITERS, 12)),
+        pltpu.SemaphoreType.DMA((13,)), pltpu.SemaphoreType.DMA((ITERS, 12)), pltpu.SemaphoreType.DMA((ITERS, 12)),
     ]
     updated, residual = pl.pallas_call(
         kernel,
         out_shape=(jax.ShapeDtypeStruct(flat, F32), jax.ShapeDtypeStruct(flat, F32)),
         in_specs=[hbm] * 13,
-        out_specs=(hbm, hbm),
+        out_specs=(vmem, vmem),
         scratch_shapes=scratch,
-        compiler_params=pltpu.CompilerParams(collective_id=0, has_side_effects=True),
+        compiler_params=pltpu.CompilerParams(collective_id=0, has_side_effects=True, vmem_limit_bytes=24 * 1024 * 1024),
         name="richardson",
-    )(
+    )(*(pltpu.with_memory_space_constraint(a, pltpu.HBM) for a in (
         solution.reshape(flat), right_side.reshape(flat), span_index.reshape(flat), coef_table.reshape(1, 8),
         jnp.swapaxes(xaxis_bands, 0, 1), jnp.swapaxes(yaxis_bands, 0, 1), jnp.swapaxes(zaxis_bands, 0, 1),
         xaxis_vectors, yaxis_vectors, zaxis_vectors,
         xaxis_values.reshape(1, 512), yaxis_values.reshape(1, 256), zaxis_values.reshape(1, 256),
-    )
+    )))
     updated, residual = pl.pallas_call(
         finish,
         out_shape=(jax.ShapeDtypeStruct(flat, F32), jax.ShapeDtypeStruct(flat, F32)),
         in_specs=[vmem, vmem],
         out_specs=(vmem, vmem),
+        compiler_params=pltpu.CompilerParams(vmem_limit_bytes=8 * 1024 * 1024),
         name="finish",
     )(updated, residual)
     return updated.reshape(solution.shape), residual.reshape(solution.shape)

time: 107 us -> 103 us (0.963)
  Pallas kernels: 106 us -> 102 us
    pallas_call x1, Pallas kernels: 104 us -> 101 us  [shards(): pl.pallas_call(kernel, out_shape=(jax.ShapeDtypeStruct(flat, F32), jax.Sh...]
where the time goes in v6:
time: 103 us; the launch traced here: 102 us
  Pallas kernels  102 us (99%)
    pallas_call x1, Pallas kernels, shards(): pl.pallas_call(kernel, out_shape=(jax.ShapeDtypeStruct(flat, F32), jax.Sh...  101 us

profile of v6, /device:TPU:1, one launch (start us, length us, event | category | flops | bytes accessed | tf_op | source)
XLA Modules:
  0.0 102.4 jit_solution(17601342910935045689)
XLA Ops:
  0.6 100.9 %richardson.1 = (f32[128,512]{1,0:T(8,128)S(1)}, f32[128,512]{1,0:T(8,128)S(1)}) custom-call(f32[128,512]{1,0:T(8,128)} %bitcast.12, f32[128,512]{1,0:T(8,128)} %bitcast.13, s32[128,512]{1,0:T(8,128)} %bitcast.14, f32[1,8]{1,0:T(1,128)} %bitcast.21, f32[7,2,512]{2,1,0:T(2,128)} %bitcast.15, f32[7,2,8]{2,1,0:T(2,128)} %bitcast.16, f32[7,2,16]{2,1,0:T(2,128)} %bitcast.17, ...), custom_call_target="tpu_custom_call" | custom-call | tf_op jit(solution)/shard_map/richardson/pallas_call | solution.py:548
  101.5 0.8 finish.1

commit v7 on v6

--- a/solution.py
+++ b/solution.py
@@ -267,17 +267,17 @@
         push(it, cs.at[it, 2], hc.at[it, 1], 6, near(1, -1))
         push(it, cs.at[it, 1], hc.at[it, 2], 6, near(-1, 1))
         push(it, cs.at[it, 0], hc.at[it, 3], 6, near(-1, -1))
-
-        @pl.when(jnp.logical_not(top))
-        def _():
-            push(it, own.at[80:128], hr.at[it, 0:48], 0, near(1, 0))
-
-        @pl.when(jnp.logical_not(bottom))
-        def _():
-            push(it, own.at[0:48], hr.at[it, 48:96], 0, near(-1, 0))
-
         push(it, zs.at[it, 1], hr.at[it, 96:120], 0, near(0, 1))
         push(it, zs.at[it, 0], hr.at[it, 120:144], 0, near(0, -1))
+
+        @pl.when(jnp.logical_not(top))
+        def _():
+            push(it, own.at[80:128], hr.at[it, 0:48], 0, near(1, 0))
+
+        @pl.when(jnp.logical_not(bottom))
+        def _():
+            push(it, own.at[0:48], hr.at[it, 48:96], 0, near(-1, 0))
+
 
     def relay(it):
         @pl.when(jnp.logical_not(top | bottom))
@@ -529,15 +529,15 @@
     hbm = pl.BlockSpec(memory_space=pl.ANY)
     vmem = pl.BlockSpec(memory_space=pltpu.VMEM)
     V = pltpu.VMEM
-    big = V((ITERS, 512, 128), F32)
-    half = V((ITERS, 256, 128), F32)
+    big = V((ITERS + 1, 512, 128), F32)
+    half = V((ITERS + 1, 256, 128), F32)
     ring = V((ITERS, 16, 32, 128), F32)
     scratch = [
         V(flat, F32), V(flat, F32), V(flat, jnp.int32), V((512, 512), F32), V((256, 256), F32), V((256, 256), F32),
         V((7, 2, 512), F32), V((7, 2, 8), F32), V((7, 2, 16), F32), V((1, 512), F32), V((1, 256), F32), V((1, 256), F32), V((1, 8), F32),
-        V(flat, F32), V(flat, F32), V((ITERS, 2, 24, 512), F32), V((ITERS, 4, 40, 128), F32),
-        V((ITERS, 4, 40, 128), F32), V((ITERS, 48, 128), F32),
-        V((ITERS, 256, 512), F32), V((ITERS, 128, 512), F32), V((256, 512), F32),
+        V(flat, F32), V(flat, F32), V((ITERS, 2, 24, 512), F32), V((ITERS + 1, 4, 40, 128), F32),
+        V((ITERS + 1, 4, 40, 128), F32), V((ITERS, 48, 128), F32),
+        V((ITERS, 256, 512), F32), V((ITERS + 1, 128, 512), F32), V((256, 512), F32),
         big, big, ring, ring, half, half, big, V((256, 256), F32), half, half, half, big, ring, ring, half, big, V((512, 128), F32),
         V((256, 384), BF16), V((256, 384), BF16), V((512, 512), BF16), V((512, 512), BF16),
         V((256, 256), BF16), V((256, 256), BF16), V((256, 256), BF16), V((256, 256), BF16),

time: 103 us -> 102 us (level)
  no operation moved by 1% of the time
where the time goes in v7:
time: 102 us
  Pallas kernels  101 us (99%)
    pallas_call x1, Pallas kernels, shards(): pl.pallas_call(kernel, out_shape=(jax.ShapeDtypeStruct(flat, F32), jax.Sh...  101 us

profile of v7, /device:TPU:1, one launch (start us, length us, event | category | flops | bytes accessed | tf_op | source)
XLA Modules:
  0.0 102.1 jit_solution(3485436477044291274)
XLA Ops:
  0.6 100.6 %richardson.1 = (f32[128,512]{1,0:T(8,128)S(1)}, f32[128,512]{1,0:T(8,128)S(1)}) custom-call(f32[128,512]{1,0:T(8,128)} %bitcast.12, f32[128,512]{1,0:T(8,128)} %bitcast.13, s32[128,512]{1,0:T(8,128)} %bitcast.14, f32[1,8]{1,0:T(1,128)} %bitcast.21, f32[7,2,512]{2,1,0:T(2,128)} %bitcast.15, f32[7,2,8]{2,1,0:T(2,128)} %bitcast.16, f32[7,2,16]{2,1,0:T(2,128)} %bitcast.17, ...), custom_call_target="tpu_custom_call" | custom-call | tf_op jit(solution)/shard_map/richardson/pallas_call | solution.py:548
  101.3 0.8 finish.1
